TPU v7x, 256 devices: a whole 4x4x8 slice. The times are simulated.
256 devices in a mesh: row: 16 (over z, core), col: 16 (over x, y).
Axes of the slice: x: 4, y: 4, z: 8, core: 2. Of those that a mesh axis runs over, the one named last changes fastest.
Arguments:
- factor: float32 [1, 16, 896, 1, 16, 896], P(None, 'row', None, None, 'col'), as said below
- damping: float32 [1], replicated, may hold values from 0.1 to 1
Outputs:
- factor_state: float32 [1, 16, 896, 1, 16, 896], P(None, 'row', None, None, 'col')
Inputs may be any that keep to these rules, and one draw needn't show every extreme that they name: factor is symmetric and positive semidefinite, so that A's smallest eigenvalue is at least damping[0].
All inputs are finite; a program needn't handle non-finite values.
Results may differ from a plain program's by a relative error of at most 0.00016.
Values sent between devices are 32-bit elements; how exact they have to be, the bound alone decides.
No kernel may reach another device: no remote copies, remote signals or barrier semaphores. Data moves between devices by JAX's collectives and lax.ppermute only.
A program may use at most 128 MiB of HBM per device.

v0:
```python
import jax
import jax.numpy as jnp
from jax import lax
from jax.sharding import PartitionSpec as P


def broadcast(array, axis, root):
    mine = lax.axis_index(axis) == root
    return lax.psum(jnp.where(mine, array, jnp.zeros_like(array)), axis)


def times_transposed(left, right):
    return lax.dot_general(
        left,
        right,
        (((1,), (1,)), ((), ())),
        precision=lax.Precision.HIGHEST,
        preferred_element_type=jnp.float32,
    )


def on_device(factor, damping):
    grid_rows = lax.axis_size("row")
    grid_cols = lax.axis_size("col")
    row_index = lax.axis_index("row")
    col_index = lax.axis_index("col")
    tile_rows = factor.shape[0]
    tile_cols = factor.shape[3]
    tile_order = factor.shape[2]
    strip_rows = tile_order // grid_cols
    first_axis = lax.broadcasted_iota(jnp.int32, (tile_order, tile_order), 0)
    second_axis = lax.broadcasted_iota(jnp.int32, (tile_order, tile_order), 1)
    identity = (first_axis == second_axis).astype(jnp.float32)
    empty = jnp.zeros((tile_order, tile_order), jnp.float32)
    row_ids = [0 + row_index]
    col_ids = [0 + col_index]
    tiles = [
        [factor[0, 0, :, 0, 0, :] + jnp.where(row_ids[0] == col_ids[0], damping[0], 0.0) * identity]
    ]

    def factor_tile(square):
        lower = jnp.linalg.cholesky(square)
        return (lower, jax.scipy.linalg.solve_triangular(lower, identity, lower=True))

    def skip_factor(square):
        return (empty, empty)

    def solve_all(blocks, inverse):
        return jnp.stack([times_transposed(blocks[0], inverse)])

    def solve_none(blocks, inverse):
        return jnp.zeros_like(blocks)

    panels = []

    def apply_panel(square, row_slot, col_slot, panel_id):
        return square - times_transposed(
            panels[panel_id][0][row_slot], panels[panel_id][1][col_slot]
        )

    home_row = 0 % grid_rows
    home_col = 0 % grid_cols
    slot_row = 0 // grid_rows
    slot_col = 0 // grid_cols
    is_home = jnp.logical_and(row_index == home_row, col_index == home_col)
    in_panel = col_index == home_col
    diag_lower, diag_inverse = lax.cond(
        is_home, factor_tile, skip_factor, tiles[slot_row][slot_col]
    )
    own_blocks = jnp.stack([tiles[0][slot_col]])
    inverse_here = broadcast(diag_inverse, "row", home_row)
    solved_own = lax.cond(in_panel, solve_all, solve_none, own_blocks, inverse_here)
    outgoing = jnp.stack(
        [jnp.where(row_ids[0] > 0, solved_own[0], jnp.where(row_ids[0] == 0, diag_lower, 0.0))]
    )
    strips = lax.all_to_all(outgoing, "col", split_axis=1, concat_axis=1, tiled=True)
    home_strip = lax.slice_in_dim(
        strips, home_col * strip_rows, (home_col + 1) * strip_rows, axis=1
    )
    arrived = lax.all_gather(home_strip, "col", axis=1, tiled=True)
    row_slot = 0
    tiles[row_slot][slot_col] = jnp.where(in_panel, arrived[row_slot], tiles[row_slot][slot_col])
    col_slot = 0
    wanted = col_ids[col_slot]
    source_slot = wanted // grid_rows
    piece_here = lax.dynamic_index_in_dim(arrived, source_slot, 0, keepdims=False)
    col_pieces = [broadcast(piece_here, "row", wanted % grid_rows)]
    panels.append((arrived, col_pieces))
    row_slot = 0
    col_slot = 0
    chosen = jnp.logical_and(row_ids[row_slot] >= col_ids[col_slot], col_ids[col_slot] > 0)
    tiles[row_slot][col_slot] = lax.cond(
        chosen,
        lambda square, rs=row_slot, cs=col_slot, pid=0: apply_panel(square, rs, cs, pid),
        lambda square: square,
        tiles[row_slot][col_slot],
    )
    row_slot = 0
    kept = [jnp.where(row_ids[row_slot] >= col_ids[0], tiles[row_slot][0], 0.0)]
    finished = [jnp.stack(kept, axis=1)]
    stacked = jnp.stack(finished, axis=0)
    return stacked.reshape(tile_rows, 1, tile_order, tile_cols, 1, tile_order)


def solution(mesh):
    return jax.shard_map(
        on_device,
        mesh=mesh,
        in_specs=(P(None, "row", None, None, "col", None), P()),
        out_specs=P(None, "row", None, None, "col", None),
        check_vma=False,
    )
```

profile of v0, /device:TPU:9, one launch (start us, length us, event | category | flops | bytes accessed | tf_op | source)
XLA Modules:
  0.0 705.8 jit_solution(6807811891235126774)
XLA Ops:
  6.5 0.0 all-reduce.4.cloned.1.call-start
  6.5 1.9 fusion.69
  9.1 2.1 bitcast_add_fusion.1
  11.2 10.6 %conditional.3 = (f32[896,896]{1,0:T(8,128)}, f32[896,896]{1,0:T(8,128)}) conditional(s32[]{:T(128)} %convert_element_type.26, () %tuple.28, (f32[896,896]{1,0:T(8,128)S(1)}, f32[896,896]{1,0:T(8,128)}, f32[896,896]{1,0:T(8,128)}, f32[896,896]{1,0:T(8,128)}, f32[896,896]{1,0:T(8,128)}, /*index=5*/f32[896,896]{1,0:T(8,128)}, f32[896,896]{1,0:T(8,128)}, ...), branch_computations={%region_0.1_spmd, %region_1.16_spmd} | conditional | flops 6878954496 | bytes 101458848 | solution.py:67
  11.2 1.9 broadcast.318
  13.2 1.9 broadcast.318.clone
  21.9 1.9 broadcast_select_fusion
  23.8 0.0 all-reduce.4.cloned.1.call-update
  23.8 0.0 all-gather.2.cloned.1.call-start
  23.9 416.9 %all-reduce.4.cloned.1.call-done = f32[896,896]{1,0:T(8,128)} async-done(((f32[896,896]{1,0:T(8,128)}), f32[896,896]{1,0:T(8,128)}) %all-reduce.4.cloned.1.call-update) | async-done | bytes 3211280 | tf_op jit(solution)/shard_map/psum | solution.py:9
  440.8 1.9 conditional.4
  440.8 1.9 squeeze.14
  442.7 2.2 select_select_fusion.1
  444.9 4.7 stack.4
  449.7 53.7 %all_to_all.5 = f32[1,896,896]{2,0,1:T(1,128)S(1)} all-to-all(f32[1,896,896]{2,0,1:T(1,128)S(1)} %stack.4), channel_id=1, replica_groups=mesh['row'=16,'col'=16] {'col'}, dimensions={1} | all-to-all | bytes 6422528 | tf_op jit(solution)/shard_map/all_to_all | solution.py:76
  503.4 0.1 slice.228
  503.4 0.7 copy.10
  504.1 0.0 all-gather.2.cloned.1.call-update
  504.2 0.0 all-reduce.6.cloned.1.call-start
  504.2 49.1 %all-gather.2.cloned.1.call-done = f32[1,896,896]{2,1,0:T(8,128)} async-done(((f32[1,56,896]{2,1,0:T(8,128)}), f32[1,896,896]{2,1,0:T(8,128)}) %all-gather.2.cloned.1.call-update) | async-done | bytes 3211280 | tf_op jit(solution)/shard_map/all_gather | solution.py:80
  553.3 5.3 bitcast_select_fusion
  558.6 0.0 all-reduce.6.cloned.1.call-update
  558.6 119.2 %all-reduce.6.cloned.1.call-done = f32[896,896]{1,0:T(8,128)} async-done(((f32[896,896]{1,0:T(8,128)}), f32[896,896]{1,0:T(8,128)}) %all-reduce.6.cloned.1.call-update) | async-done | bytes 3211280 | tf_op jit(solution)/shard_map/psum | solution.py:9
  677.8 16.0 %conditional.5 = (f32[896,896]{1,0:T(8,128)S(1)}) conditional(s32[]{:T(128)} %convert_element_type.24, f32[896,896]{1,0:T(8,128)S(1)} %get-tuple-element.131, (f32[1,896,896]{2,1,0:T(8,128)}, f32[896,896]{1,0:T(8,128)}, f32[896,896]{1,0:T(8,128)S(1)}) %tuple.31), branch_computations={%region_20.21_spmd, %region_21.22_spmd} | conditional | flops 8632680448 | bytes 12845064 | solution.py:92
  678.2 15.5 %fusion.2 = f32[896,896]{1,0:T(8,128)S(1)} fusion(f32[896,896]{1,0:T(8,128)S(1)} %get-tuple-element.43, f32[896,896]{1,0:T(8,128)} %get-tuple-element.45, f32[1,896,896]{2,1,0:T(8,128)} %get-tuple-element.44), kind=kOutput, calls=%fused_computation.2 | convolution fusion | flops 8632680448 | bytes 12845056 | tf_op jit(solution)/shard_map/cond/branch_1_fun/dot_general | solution.py:13
  693.9 0.2 select_bitcast_fusion.6
  694.1 5.0 copy.8
Async XLA Ops:
  6.5 434.2 %all-reduce.4.cloned.1.call-start = ((), (), s32[]{:S(2)}) async-start(), calls=%async_computation.1 | async-start | bytes 6422528 | tf_op jit(solution)/shard_map/psum | solution.py:9
  23.8 529.5 %all-gather.2.cloned.1.call-start = ((), (), s32[]{:S(2)}) async-start(), calls=%async_computation.2 | async-start | bytes 3411968 | tf_op jit(solution)/shard_map/all_gather | solution.py:80
  504.2 173.7 %all-reduce.6.cloned.1.call-start = ((), (), s32[]{:S(2)}) async-start(), calls=%async_computation.3 | async-start | bytes 6422528 | tf_op jit(solution)/shard_map/psum | solution.py:9
Sparse Core Ops, SparseCore 0:
  23.9 416.7 all-reduce.3
  504.3 48.9 all-gather.1
  558.7 119.0 all-reduce.5
where the time goes:
time: 717 us; the launch traced here: 706 us
  waiting for transfers between devices  585 us (82%)
  blocking collectives  53.7 us (7%)
  local copies, waits for them, and re-layouts  16.2 us (2%)
  matrix products  15.5 us (2%)
  between operations  14 us (2%)
  other arithmetic  13.7 us (2%)
  loops' own time  7.36 us (1%)
    psum x2, waiting for transfers between devices, broadcast(): return lax.psum(jnp.where(mine, array, jnp.zeros_like(array)), axis)  536 us
    all_to_all x1, blocking collectives, on_device(): lax.all_to_all(outgoing, 'col', split_axis=1, concat_axis=1, tiled=True)  53.7 us
    all_gather x1, waiting for transfers between devices, on_device(): arrived = lax.all_gather(home_strip, 'col', axis=1, tiled=True)  49.1 us
    dot_general x1, matrix products, times_transposed(): lax.dot_general(left, right, (((1,), (1,)), ((), ())), precision=lax.Prec...  15.5 us
  transfers between devices with their start and end apart: 3, of which 3 were waited for; matrix products, arithmetic and copies ran while one was open for 0% of the time, Pallas kernels for 0%

commit v1 on v0

v1 whole, which is shorter than its diff:
```python
import jax
import jax.numpy as jnp
from jax import lax
from jax.experimental import pallas as pl
from jax.experimental.pallas import tpu as pltpu
from jax.sharding import PartitionSpec as P

F32 = jnp.float32
BF16 = jnp.bfloat16
ORDER = 896
LANES = 128
BLOCKS = ORDER // LANES
FLAT = ORDER * BLOCKS
GRID = 16
PIECE = FLAT // GRID
GROUPS = ((0, 256), (256, 512), (512, 768), (768, 896))
INTERPRET = False


def split(value):
    high = value.astype(BF16)
    return high, (value - high.astype(F32)).astype(BF16)


def product(left, right, transposed):
    dims = (((1,), (1 if transposed else 0,)), ((), ()))
    return lax.dot_general(left, right, dims, preferred_element_type=F32)


def product3(left, right, transposed=False):
    (left_high, left_low), (right_high, right_low) = left, right
    return product(left_high, right_high, transposed) + (
        product(left_high, right_low, transposed) + product(left_low, right_high, transposed)
    )


def factor_block(rows):
    lane = lax.broadcasted_iota(jnp.int32, (8, LANES), 1)
    sublane = lax.broadcasted_iota(jnp.int32, (8, LANES), 0)

    def lane_of(value, index):
        return jnp.broadcast_to(value[:, index:index + 1], (8, LANES))

    def row_of(value, index):
        return jnp.broadcast_to(value[index:index + 1, :], (8, LANES))

    rows = list(rows)
    mixed, corner = [], []
    for slab in range(16):
        base = 8 * slab
        own = (lane >= base) & (lane < base + 8)
        pivot_rows = rows[slab]
        columns = [lane_of(pivot_rows, base + m) for m in range(8)]
        diag_rows = jnp.where(own, pivot_rows, 0.0)
        pivot_rows = jnp.where(own, jnp.where(lane - base == sublane, 1.0, 0.0), pivot_rows)
        mixed_slab = jnp.zeros((8, LANES), F32)
        corner_slab = jnp.zeros((8, LANES), F32)
        for j in range(8):
            pivot = row_of(columns[j], j)
            root = lax.rsqrt(pivot)
            inverse = 1.0 / pivot
            is_j = sublane == j
            factor = jnp.where(is_j, 1.0 - inverse, columns[j] * inverse)
            mixed_slab = jnp.where(is_j, pivot_rows * root, mixed_slab)
            corner_slab = jnp.where(is_j, diag_rows * root, corner_slab)
            for m in range(j + 1, 8):
                columns[m] = columns[m] - factor * row_of(columns[m], j)
            pivot_rows = pivot_rows - factor * row_of(pivot_rows, j)
            if j < 7:
                diag_rows = diag_rows - factor * row_of(diag_rows, j)
        mixed.append(mixed_slab)
        corner.append(corner_slab)
        spread = [row_of(pivot_rows, m) for m in range(8)]
        for other in range(slab + 1, 16):
            old = rows[other]
            new = jnp.where(own, 0.0, old)
            for m in range(8):
                new = new - lane_of(old, base + m) * spread[m]
            rows[other] = new
    return mixed, corner


def factor_kernel(damping_ref, tile_ref, high_ref, low_ref, upper_ref, work):
    damping = damping_ref[0]
    row_id = lax.broadcasted_iota(jnp.int32, (ORDER, LANES), 0)
    lane_id = lax.broadcasted_iota(jnp.int32, (ORDER, LANES), 1)
    for block in range(BLOCKS):
        values = tile_ref[pl.ds(block, ORDER, stride=BLOCKS), :]
        on_diagonal = row_id == lane_id + LANES * block
        work[:, LANES * block:LANES * (block + 1)] = jnp.where(on_diagonal, values + damping, values)
    lane = lax.broadcasted_iota(jnp.int32, (8, LANES), 1)

    def step(k, carry):
        start = pl.multiple_of(k * LANES, LANES)
        here = pl.ds(start, LANES)
        slabs = [work[pl.ds(start + 8 * i, 8), here] for i in range(16)]
        mixed, corner = factor_block(slabs)
        inverse = jnp.concatenate([jnp.where(lane < 8 * i + 8, mixed[i], 0.0) for i in range(16)], axis=0)
        upper = jnp.concatenate([jnp.where(lane < 8 * i + 8, corner[i], mixed[i]) for i in range(16)], axis=0)
        inverse_parts = split(inverse)
        work[here, :] = product3(inverse_parts, split(work[here, :]))
        upper_ref[here, :] = work[here, :]
        upper_ref[here, here] = upper
        work[here, here] = inverse
        panel_parts = split(work[here, :])

        def update(i, inner):
            there = pl.ds(pl.multiple_of(i * LANES, LANES), LANES)
            column = product3(split(work[there, here]), inverse_parts, transposed=True)
            work[there, here] = jnp.zeros((LANES, LANES), F32)
            work[there, :] = work[there, :] - product3(split(column), panel_parts)
            return inner

        lax.fori_loop(k + 1, BLOCKS, update, 0)
        return carry

    lax.fori_loop(0, BLOCKS, step, 0)
    for i in range(BLOCKS):
        down = slice(LANES * i, LANES * (i + 1))
        row_id = lax.broadcasted_iota(jnp.int32, (LANES, ORDER), 0) + LANES * i
        col_id = lax.broadcasted_iota(jnp.int32, (LANES, ORDER), 1)
        high, low = split(jnp.where(col_id <= row_id, work[down, :], 0.0))
        high_ref[down, :] = high
        low_ref[down, :] = low


def update_kernel(
    where_ref, damping_ref, high_ref, low_ref, upper_ref, row_ref, col_ref, own_ref, out_ref,
    row_high, row_low, col_high, col_low, left_high, left_low,
):
    row, col = where_ref[0], where_ref[1]

    def load(ref, high, low):
        for block in range(BLOCKS):
            lanes = slice(LANES * block, LANES * (block + 1))
            high[:, lanes], low[:, lanes] = split(ref[pl.ds(block, ORDER, stride=BLOCKS), :])

    @pl.when(row < col)
    def _():
        out_ref[...] = jnp.zeros((FLAT, LANES), F32)

    @pl.when(jnp.logical_and(row == 0, col == 0))
    def _():
        row_id = lax.broadcasted_iota(jnp.int32, (ORDER, LANES), 0)
        lane_id = lax.broadcasted_iota(jnp.int32, (ORDER, LANES), 1)
        for block in range(BLOCKS):
            lower = upper_ref[LANES * block:LANES * (block + 1), :].T
            keep = row_id >= lane_id + LANES * block
            out_ref[pl.ds(block, ORDER, stride=BLOCKS), :] = jnp.where(keep, lower, 0.0)

    @pl.when(jnp.logical_and(row > 0, col == 0))
    def _():
        load(own_ref, row_high, row_low)
        for start, stop in GROUPS:
            left = row_high[:, :stop], row_low[:, :stop]
            result = product3(left, (high_ref[start:stop, :stop], low_ref[start:stop, :stop]), transposed=True)
            for block in range(start // LANES, stop // LANES):
                at = LANES * block - start
                out_ref[pl.ds(block, ORDER, stride=BLOCKS), :] = result[:, at:at + LANES]

    @pl.when(jnp.logical_and(row >= col, col > 0))
    def _():
        load(row_ref, row_high, row_low)
        load(col_ref, col_high, col_low)
        for start, stop in reversed(GROUPS):
            weights = high_ref[start:stop, :stop], low_ref[start:stop, :stop]
            solved = product3(weights, (row_high[:stop, :], row_low[:stop, :]))
            left_high[:, start:stop], left_low[:, start:stop] = split(solved.T)
            solved = product3(weights, (col_high[:stop, :], col_low[:stop, :]))
            col_high[start:stop, :], col_low[start:stop, :] = split(solved)
        added = jnp.where(row == col, damping_ref[0], 0.0)
        row_id = lax.broadcasted_iota(jnp.int32, (ORDER, LANES), 0)
        lane_id = lax.broadcasted_iota(jnp.int32, (ORDER, LANES), 1)
        for start, stop in GROUPS:
            left = left_high[...], left_low[...]
            result = product3(left, (col_high[:, start:stop], col_low[:, start:stop]))
            for block in range(start // LANES, stop // LANES):
                at = LANES * block - start
                place = pl.ds(block, ORDER, stride=BLOCKS)
                own = own_ref[place, :]
                own = jnp.where(row_id == lane_id + LANES * block, own + added, own)
                out_ref[place, :] = own - result[:, at:at + LANES]


VMEM = pl.BlockSpec(memory_space=pltpu.VMEM)
SMEM = pl.BlockSpec(memory_space=pltpu.SMEM)


def factorize(damping, tile):
    return pl.pallas_call(
        factor_kernel,
        out_shape=[
            jax.ShapeDtypeStruct((ORDER, ORDER), BF16),
            jax.ShapeDtypeStruct((ORDER, ORDER), BF16),
            jax.ShapeDtypeStruct((ORDER, ORDER), F32),
        ],
        in_specs=[SMEM, VMEM],
        out_specs=[VMEM, VMEM, VMEM],
        scratch_shapes=[pltpu.VMEM((ORDER, ORDER), F32)],
        interpret=INTERPRET,
        name="factorize",
    )(damping, tile)


def finish(where, damping, high, low, upper, row_tile, col_tile, own):
    return pl.pallas_call(
        update_kernel,
        out_shape=jax.ShapeDtypeStruct((FLAT, LANES), F32),
        in_specs=[SMEM, SMEM] + [VMEM] * 6,
        out_specs=VMEM,
        scratch_shapes=[pltpu.VMEM((ORDER, ORDER), BF16)] * 6,
        interpret=INTERPRET,
        name="finish",
    )(where, damping, high, low, upper, row_tile, col_tile, own)


def on_device(factor, damping):
    row = lax.axis_index("row")
    col = lax.axis_index("col")
    own = factor.reshape(FLAT, LANES)

    piece = jnp.where(row == 0, own[:PIECE], 0.0)
    arrived = [
        lax.ppermute(own[PIECE * r:PIECE * (r + 1)], "row", [(0, r)]) for r in range(1, GRID)
    ]
    for other in arrived:
        piece = piece + other

    first = jnp.where(col == 0, piece, 0.0)
    for hop in (8, 4, 2, 1):
        pairs = [(c, c + hop) for c in range(0, GRID, 2 * hop)]
        first = first + lax.ppermute(first, "col", pairs)

    swap = [(r * GRID + c, c * GRID + r) for r in range(GRID) for c in range(GRID)]
    turned = lax.ppermute(piece, ("row", "col"), swap)

    col_tile = lax.all_gather(piece, "row", axis=0, tiled=True)
    first_tile = lax.all_gather(first, "row", axis=0, tiled=True)
    row_tile = lax.all_gather(turned, "col", axis=0, tiled=True)

    high, low, upper = factorize(damping, first_tile)
    where = jnp.stack([row, col]).astype(jnp.int32)
    result = finish(where, damping, high, low, upper, row_tile, col_tile, own)
    return result.reshape(factor.shape)


def solution(mesh):
    return jax.shard_map(
        on_device,
        mesh=mesh,
        in_specs=(P(None, "row", None, None, "col", None), P()),
        out_specs=P(None, "row", None, None, "col", None),
        check_vma=False,
    )
```

time: 717 us -> 244 us (0.34); the launches traced: 706 us -> 243 us
  waiting for transfers between devices: 585 us -> 128 us
  Pallas kernels: 0 us -> 74 us
  blocking collectives: 53.7 us -> 0 us
  starting transfers between devices: 0.08 us -> 18.3 us
  matrix products: 15.5 us -> 0 us
  local copies, waits for them, and re-layouts: 16.2 us -> 0.7 us
  loops' own time: 7.36 us -> 0 us
    psum x2 -> x0, waiting for transfers between devices: 536 us -> none  [broadcast(): return lax.psum(jnp.where(mine, array, jnp.zeros_like(array)), axis)]
    pallas_call x0 -> x2, Pallas kernels: none -> 74 us  [the longest x1 53.2 us: factorize(): pl.pallas_call(factor_kernel, out_shape=[jax.ShapeDtypeStruct((ORDER, ORD...]
    all_gather x1 -> x3, waiting for transfers between devices: 49.1 us -> 111 us  [the longest x1 66.9 us: on_device(): first_tile = lax.all_gather(first, 'row', axis=0, tiled=True)]
    all_to_all x1 -> x0, blocking collectives: 53.7 us -> none  [on_device(): lax.all_to_all(outgoing, 'col', split_axis=1, concat_axis=1, tiled=True)]
    ppermute x0 -> x20, starting transfers between devices: none -> 18.3 us  [the longest x15 13.4 us: on_device(): lax.ppermute(own[PIECE * r:PIECE * (r + 1)], 'row', [(0, r)])]
    ppermute x0 -> x20, waiting for transfers between devices: none -> 16.4 us  [the longest x4 16.3 us: on_device(): first = first + lax.ppermute(first, 'col', pairs)]
    dot_general x1 -> x0, matrix products: 15.5 us -> none  [times_transposed(): lax.dot_general(left, right, (((1,), (1,)), ((), ())), precision=lax.Prec...]
    another operation x4 -> x0, local copies, waits for them, and re-layouts: 13.6 us -> none  [the longest x1 4.99 us: on_device(): return stacked.reshape(tile_rows, 1, tile_order, tile_cols, 1, tile_order)]
  transfers between devices with their start and end apart: 3 -> 23, of which waited for: 3 -> 3; matrix products, arithmetic and copies ran while one was open for 0% -> 0% of each run, Pallas kernels for 0% -> 22%
where the time goes in v1:
time: 244 us; the launch traced here: 243 us
  waiting for transfers between devices  128 us (52%)
  Pallas kernels  74 us (30%)
  starting transfers between devices  18.3 us (8%)
  between operations  14 us (6%)
  other arithmetic  7.66 us (3%)
    all_gather x1, waiting for transfers between devices, on_device(): first_tile = lax.all_gather(first, 'row', axis=0, tiled=True)  66.9 us
    pallas_call x1, Pallas kernels, factorize(): pl.pallas_call(factor_kernel, out_shape=[jax.ShapeDtypeStruct((ORDER, ORD...  53.2 us
    all_gather x1, waiting for transfers between devices, on_device(): row_tile = lax.all_gather(turned, 'col', axis=0, tiled=True)  44.1 us
    pallas_call x1, Pallas kernels, finish(): pl.pallas_call(update_kernel, out_shape=jax.ShapeDtypeStruct((FLAT, LANES...  20.8 us
    ppermute x4, waiting for transfers between devices, on_device(): first = first + lax.ppermute(first, 'col', pairs)  16.3 us
    ppermute x15, starting transfers between devices, on_device(): lax.ppermute(own[PIECE * r:PIECE * (r + 1)], 'row', [(0, r)])  13.4 us
  transfers between devices with their start and end apart: 23, of which 3 were waited for; matrix products, arithmetic and copies ran while one was open for 0% of the time, Pallas kernels for 22%

profile of v1, /device:TPU:9, one launch (start us, length us, event | category | flops | bytes accessed | tf_op | source)
XLA Modules:
  0.0 242.9 jit_solution(7850023057511235947)
XLA Ops:
  6.5 4.1 %fusion = (f32[1,1,56,1,1,896]{5,4,3,2,1,0:T(1,128)S(1)}, f32[1,1,56,1,1,896]{5,4,3,2,1,0:T(1,128)S(1)}, f32[1,1,56,1,1,896]{5,4,3,2,1,0:T(1,128)S(1)}, f32[1,1,...) fusion(f32[1,1,896,1,1,896]{5,4,3,2,1,0:T(1,128)} %param.2, ...), kind=kLoop, calls=%fused_computation.4 | loop fusion | flops 50176 | bytes 6422529 | tf_op jit(solution)/shard_map/slice | solution.py:224
  10.6 1.3 collective-permute-start
  11.9 0.7 collective-permute-start.1
  12.6 0.7 collective-permute-start.10
  13.3 0.7 collective-permute-start.11
  14.0 0.7 collective-permute-start.12
  14.7 0.7 collective-permute-start.13
  15.3 0.7 collective-permute-start.14
  16.0 0.7 collective-permute-start.2
  16.7 0.7 collective-permute-start.3
  17.4 0.7 collective-permute-start.4
  18.1 0.7 collective-permute-start.5
  18.8 1.3 collective-permute-start.6
  20.2 1.3 collective-permute-start.7
  21.5 1.3 collective-permute-start.8
  22.8 1.3 collective-permute-start.9
  24.2 2.2 broadcast_select_fusion.1
  26.4 0.7 collective-permute-start.15
  27.1 0.7 collective-permute-start.16
  27.8 0.7 collective-permute-start.17
  28.5 1.3 collective-permute-start.18
  29.8 16.3 %collective-permute-done.18 = f32[392,128]{1,0:T(8,128)S(1)} collective-permute-done((f32[392,128]{1,0:T(8,128)S(1)}, f32[392,128]{1,0:T(8,128)S(1)}, u32[]{:S(2)}, u32[]{:S(2)}) %collective-permute-start.18) | collective-permute-done | bytes 200736 | tf_op jit(solution)/shard_map/ppermute | solution.py:232
  46.2 0.7 add.75
  46.9 0.0 all-gather.8.cloned.1.call-start
  46.9 0.7 all-gather.8.cloned.1.call-update
  47.7 1.6 collective-permute-start.19
  49.3 0.7 copy-done
  50.7 0.6 pad_add_fusion.where_ref
  51.3 66.9 %all-gather.4.cloned.1.call-done.tile_ref = f32[6272,128]{1,0:T(8,128)} async-done(((f32[392,128]{1,0:T(8,128)}), f32[6272,128]{1,0:T(8,128)}) %all-gather.4.cloned.1.call-update) | async-done | bytes 3211280 | tf_op jit(solution)/shard_map/all_gather | solution.py:238
  118.2 53.2 %factorize.1 = (bf16[896,896]{1,0:T(8,128)(2,1)}, bf16[896,896]{1,0:T(8,128)(2,1)}, f32[896,896]{1,0:T(8,128)}) custom-call(f32[1]{0:T(128)S(6)} %copy.4.damping_ref, f32[6272,128]{1,0:T(8,128)} %all-gather.4.cloned.1.call-done.tile_ref), custom_call_target="tpu_custom_call" | custom-call | tf_op jit(solution)/shard_map/factorize/pallas_call | solution.py:190
  171.4 44.1 %all-gather.6.cloned.1.call-done.row_ref = f32[6272,128]{1,0:T(8,128)} async-done(((f32[392,128]{1,0:T(8,128)}), f32[6272,128]{1,0:T(8,128)}) %all-gather.6.cloned.1.call-update) | async-done | bytes 3211280 | tf_op jit(solution)/shard_map/all_gather | solution.py:239
  215.5 20.8 %finish.1 = f32[6272,128]{1,0:T(8,128)} custom-call(s32[2]{0:T(128)} %pad_add_fusion.where_ref, f32[1]{0:T(128)S(6)} %copy.4.damping_ref, bf16[896,896]{1,0:T(8,128)(2,1)} %get-tuple-element.8.high_ref, bf16[896,896]{1,0:T(8,128)(2,1)} %get-tuple-element.9.low_ref, f32[896,896]{1,0:T(8,128)} %get-tuple-element.10.upper_ref, ...), custom_call_target="tpu_custom_call" | custom-call | tf_op jit(solution)/shard_map/finish/pallas_call | solution.py:206
  (28 shorter events, 0.2 us)
Async XLA Ops:
  6.5 111.7 %all-gather.4.cloned.1.call-start = ((), (), s32[]{:S(2)}) async-start(), calls=%async_computation | async-start | bytes 3411968 | tf_op jit(solution)/shard_map/all_gather | solution.py:238
  10.6 4.0 %collective-permute-start = (f32[392,128]{1,0:T(8,128)S(1)}, f32[392,128]{1,0:T(8,128)S(1)}, u32[]{:S(2)}, u32[]{:S(2)}) collective-permute-start(f32[392,128]{1,0:T(8,128)S(1)} %bitcast.36), channel_id=1, source_target_pairs={{0,16},{1,17},{2,18},{3,19},{4,20},{5,21},{6,22},{7,23},{8,24},{9,... | collective-permute-start | bytes 602120 | tf_op jit(solution)/shard_map/ppermute | solution.py:224
  11.9 3.4 %collective-permute-start.1 = (f32[392,128]{1,0:T(8,128)S(1)}, f32[392,128]{1,0:T(8,128)S(1)}, u32[]{:S(2)}, u32[]{:S(2)}) collective-permute-start(f32[392,128]{1,0:T(8,128)S(1)} %bitcast.35), channel_id=1, source_target_pairs={{0,32},{1,33},{2,34},{3,35},{4,36},{5,37},{6,38},{7,39},{8,40},{9,... | collective-permute-start | bytes 602120 | tf_op jit(solution)/shard_map/ppermute | solution.py:224
  12.6 3.4 %collective-permute-start.10 = (f32[392,128]{1,0:T(8,128)S(1)}, f32[392,128]{1,0:T(8,128)S(1)}, u32[]{:S(2)}, u32[]{:S(2)}) collective-permute-start(f32[392,128]{1,0:T(8,128)S(1)} %bitcast.34), channel_id=1, source_target_pairs={{0,176},{1,177},{2,178},{3,179},{4,180},{5,181},{6,182},{7,183},{8... | collective-permute-start | bytes 602120 | tf_op jit(solution)/shard_map/ppermute | solution.py:224
  13.3 3.4 %collective-permute-start.11 = (f32[392,128]{1,0:T(8,128)S(1)}, f32[392,128]{1,0:T(8,128)S(1)}, u32[]{:S(2)}, u32[]{:S(2)}) collective-permute-start(f32[392,128]{1,0:T(8,128)S(1)} %bitcast.33), channel_id=1, source_target_pairs={{0,192},{1,193},{2,194},{3,195},{4,196},{5,197},{6,198},{7,199},{8... | collective-permute-start | bytes 602120 | tf_op jit(solution)/shard_map/ppermute | solution.py:224
  14.0 3.5 %collective-permute-start.12 = (f32[392,128]{1,0:T(8,128)S(1)}, f32[392,128]{1,0:T(8,128)S(1)}, u32[]{:S(2)}, u32[]{:S(2)}) collective-permute-start(f32[392,128]{1,0:T(8,128)S(1)} %bitcast.32), channel_id=1, source_target_pairs={{0,208},{1,209},{2,210},{3,211},{4,212},{5,213},{6,214},{7,215},{8... | collective-permute-start | bytes 602120 | tf_op jit(solution)/shard_map/ppermute | solution.py:224
  14.7 3.5 %collective-permute-start.13 = (f32[392,128]{1,0:T(8,128)S(1)}, f32[392,128]{1,0:T(8,128)S(1)}, u32[]{:S(2)}, u32[]{:S(2)}) collective-permute-start(f32[392,128]{1,0:T(8,128)S(1)} %bitcast.31), channel_id=1, source_target_pairs={{0,224},{1,225},{2,226},{3,227},{4,228},{5,229},{6,230},{7,231},{8... | collective-permute-start | bytes 602120 | tf_op jit(solution)/shard_map/ppermute | solution.py:224
  15.3 3.5 %collective-permute-start.14 = (f32[392,128]{1,0:T(8,128)S(1)}, f32[392,128]{1,0:T(8,128)S(1)}, u32[]{:S(2)}, u32[]{:S(2)}) collective-permute-start(f32[392,128]{1,0:T(8,128)S(1)} %bitcast.30), channel_id=1, source_target_pairs={{0,240},{1,241},{2,242},{3,243},{4,244},{5,245},{6,246},{7,247},{8... | collective-permute-start | bytes 602120 | tf_op jit(solution)/shard_map/ppermute | solution.py:224
  16.0 4.1 %collective-permute-start.2 = (f32[392,128]{1,0:T(8,128)S(1)}, f32[392,128]{1,0:T(8,128)S(1)}, u32[]{:S(2)}, u32[]{:S(2)}) collective-permute-start(f32[392,128]{1,0:T(8,128)S(1)} %bitcast.29), channel_id=1, source_target_pairs={{0,48},{1,49},{2,50},{3,51},{4,52},{5,53},{6,54},{7,55},{8,56},{9,... | collective-permute-start | bytes 602120 | tf_op jit(solution)/shard_map/ppermute | solution.py:224
  16.7 4.8 %collective-permute-start.3 = (f32[392,128]{1,0:T(8,128)S(1)}, f32[392,128]{1,0:T(8,128)S(1)}, u32[]{:S(2)}, u32[]{:S(2)}) collective-permute-start(f32[392,128]{1,0:T(8,128)S(1)} %bitcast.28), channel_id=1, source_target_pairs={{0,64},{1,65},{2,66},{3,67},{4,68},{5,69},{6,70},{7,71},{8,72},{9,... | collective-permute-start | bytes 602120 | tf_op jit(solution)/shard_map/ppermute | solution.py:224
  17.4 5.4 %collective-permute-start.4 = (f32[392,128]{1,0:T(8,128)S(1)}, f32[392,128]{1,0:T(8,128)S(1)}, u32[]{:S(2)}, u32[]{:S(2)}) collective-permute-start(f32[392,128]{1,0:T(8,128)S(1)} %bitcast.27), channel_id=1, source_target_pairs={{0,80},{1,81},{2,82},{3,83},{4,84},{5,85},{6,86},{7,87},{8,88},{9,... | collective-permute-start | bytes 602120 | tf_op jit(solution)/shard_map/ppermute | solution.py:224
  18.1 6.1 %collective-permute-start.5 = (f32[392,128]{1,0:T(8,128)S(1)}, f32[392,128]{1,0:T(8,128)S(1)}, u32[]{:S(2)}, u32[]{:S(2)}) collective-permute-start(f32[392,128]{1,0:T(8,128)S(1)} %bitcast.26), channel_id=1, source_target_pairs={{0,96},{1,97},{2,98},{3,99},{4,100},{5,101},{6,102},{7,103},{8,104... | collective-permute-start | bytes 602120 | tf_op jit(solution)/shard_map/ppermute | solution.py:224
  18.8 5.4 %collective-permute-start.6 = (f32[392,128]{1,0:T(8,128)S(1)}, f32[392,128]{1,0:T(8,128)}, u32[]{:S(2)}, u32[]{:S(2)}) collective-permute-start(f32[392,128]{1,0:T(8,128)S(1)} %bitcast.25), channel_id=1, source_target_pairs={{0,112},{1,113},{2,114},{3,115},{4,116},{5,117},{6,118},{7,119},{8... | collective-permute-start | bytes 602120 | tf_op jit(solution)/shard_map/ppermute | solution.py:224
  20.2 4.0 %collective-permute-start.7 = (f32[392,128]{1,0:T(8,128)S(1)}, f32[392,128]{1,0:T(8,128)}, u32[]{:S(2)}, u32[]{:S(2)}) collective-permute-start(f32[392,128]{1,0:T(8,128)S(1)} %bitcast.24), channel_id=1, source_target_pairs={{0,128},{1,129},{2,130},{3,131},{4,132},{5,133},{6,134},{7,135},{8... | collective-permute-start | bytes 602120 | tf_op jit(solution)/shard_map/ppermute | solution.py:224
  21.5 2.7 %collective-permute-start.8 = (f32[392,128]{1,0:T(8,128)S(1)}, f32[392,128]{1,0:T(8,128)}, u32[]{:S(2)}, u32[]{:S(2)}) collective-permute-start(f32[392,128]{1,0:T(8,128)S(1)} %bitcast.23), channel_id=1, source_target_pairs={{0,144},{1,145},{2,146},{3,147},{4,148},{5,149},{6,150},{7,151},{8... | collective-permute-start | bytes 602120 | tf_op jit(solution)/shard_map/ppermute | solution.py:224
  22.8 1.4 collective-permute-start.9
  26.4 0.7 collective-permute-start.15
  27.1 0.7 collective-permute-start.16
  27.8 0.7 collective-permute-start.17
  28.5 17.6 %collective-permute-start.18 = (f32[392,128]{1,0:T(8,128)S(1)}, f32[392,128]{1,0:T(8,128)S(1)}, u32[]{:S(2)}, u32[]{:S(2)}) collective-permute-start(f32[392,128]{1,0:T(8,128)S(1)} %add.74), channel_id=1, source_target_pairs={{0,1},{2,3},{4,5},{6,7},{8,9},{10,11},{12,13},{14,15},{16,17},{18,... | collective-permute-start | bytes 602120 | tf_op jit(solution)/shard_map/ppermute | solution.py:232
  46.9 124.5 %all-gather.8.cloned.1.call-start = ((), (), s32[]{:S(2)}) async-start(), calls=%async_computation.2 | async-start | bytes 3411968 | tf_op jit(solution)/shard_map/all_gather | solution.py:237
  47.7 167.9 %all-gather.6.cloned.1.call-start = ((), (), s32[]{:S(2)}) async-start(), calls=%async_computation.1 | async-start | bytes 3411968 | tf_op jit(solution)/shard_map/all_gather | solution.py:239
  47.7 1.6 collective-permute-start.19
  49.3 0.7 copy-start
Sparse Core Ops, SparseCore 0:
  47.0 71.1 all-gather.3
  120.1 43.3 all-gather.7
  165.9 49.5 all-gather.5

commit v2 on v1

--- a/solution.py
+++ b/solution.py
@@ -12,7 +12,8 @@
 BLOCKS = ORDER // LANES
 FLAT = ORDER * BLOCKS
 GRID = 16
-PIECE = FLAT // GRID
+CHIPS = GRID // 2
+PAIR_ROWS = ORDER // CHIPS
 GROUPS = ((0, 256), (256, 512), (512, 768), (768, 896))
 INTERPRET = False
 
@@ -80,14 +81,23 @@
     return mixed, corner
 
 
-def factor_kernel(damping_ref, tile_ref, high_ref, low_ref, upper_ref, work):
+def factor_kernel(where_ref, damping_ref, *refs):
+    pair_refs, (high_ref, low_ref, upper_ref, work) = refs[:CHIPS], refs[CHIPS:]
     damping = damping_ref[0]
-    row_id = lax.broadcasted_iota(jnp.int32, (ORDER, LANES), 0)
-    lane_id = lax.broadcasted_iota(jnp.int32, (ORDER, LANES), 1)
-    for block in range(BLOCKS):
-        values = tile_ref[pl.ds(block, ORDER, stride=BLOCKS), :]
-        on_diagonal = row_id == lane_id + LANES * block
-        work[:, LANES * block:LANES * (block + 1)] = jnp.where(on_diagonal, values + damping, values)
+    chip = where_ref[0] // 2
+    sign = 1 - 2 * (where_ref[0] % 2)
+    row_id = lax.broadcasted_iota(jnp.int32, (PAIR_ROWS, LANES), 0)
+    lane_id = lax.broadcasted_iota(jnp.int32, (PAIR_ROWS, LANES), 1)
+    for index, ref in enumerate(pair_refs):
+        hop = (index + 1) // 2
+        source = (chip + (-sign if index % 2 else sign) * hop + CHIPS) % CHIPS
+        start = pl.multiple_of(source * PAIR_ROWS, PAIR_ROWS)
+        for block in range(BLOCKS):
+            values = ref[pl.ds(block, PAIR_ROWS, stride=BLOCKS), :]
+            on_diagonal = row_id + start == lane_id + LANES * block
+            work[pl.ds(start, PAIR_ROWS), LANES * block:LANES * (block + 1)] = jnp.where(
+                on_diagonal, values + damping, values
+            )
     lane = lax.broadcasted_iota(jnp.int32, (8, LANES), 1)
 
     def step(k, carry):
@@ -186,7 +196,7 @@
 SMEM = pl.BlockSpec(memory_space=pltpu.SMEM)
 
 
-def factorize(damping, tile):
+def factorize(where, damping, pairs):
     return pl.pallas_call(
         factor_kernel,
         out_shape=[
@@ -194,12 +204,12 @@
             jax.ShapeDtypeStruct((ORDER, ORDER), BF16),
             jax.ShapeDtypeStruct((ORDER, ORDER), F32),
         ],
-        in_specs=[SMEM, VMEM],
+        in_specs=[SMEM, SMEM] + [VMEM] * CHIPS,
         out_specs=[VMEM, VMEM, VMEM],
         scratch_shapes=[pltpu.VMEM((ORDER, ORDER), F32)],
         interpret=INTERPRET,
         name="factorize",
-    )(damping, tile)
+    )(where, damping, *pairs)
 
 
 def finish(where, damping, high, low, upper, row_tile, col_tile, own):
@@ -214,32 +224,53 @@
     )(where, damping, high, low, upper, row_tile, col_tile, own)
 
 
+def spread(own):
+    row = lax.axis_index("row")
+    col = lax.axis_index("col")
+    core = row % 2
+    size = own.shape[0] // GRID
+
+    piece = jnp.where(row == 0, own[:size], 0.0)
+    arrived = [
+        lax.ppermute(own[size * r:size * (r + 1)], "row", [(0, r)]) for r in range(1, GRID)
+    ]
+    for other in arrived:
+        piece = piece + other
+
+    swap = [(r * GRID + c, c * GRID + r) for r in range(GRID) for c in range(GRID)]
+    turned = lax.ppermute(piece, ("row", "col"), swap)
+    row_tile = lax.all_gather(turned, "col", axis=0, tiled=True)
+    col_tile = lax.all_gather(piece, "row", axis=0, tiled=True)
+
+    first = jnp.where(col == 0, piece, 0.0)
+    for hop in (8, 4, 2, 1):
+        pairs = [(c, c + hop) for c in range(0, GRID, 2 * hop)]
+        first = first + lax.ppermute(first, "col", pairs)
+
+    chips = GRID // 2
+    other_core = [(r, r ^ 1) for r in range(GRID)]
+    onward = [(2 * z, 2 * ((z + 1) % chips)) for z in range(chips)]
+    onward += [(2 * z + 1, 2 * ((z - 1) % chips) + 1) for z in range(chips)]
+    partner = lax.ppermute(first, "row", other_core)
+    moving = jnp.concatenate(
+        [jnp.where(core == 0, first, partner), jnp.where(core == 0, partner, first)], axis=0
+    )
+    pairs = [moving]
+    for hop in range(1, chips // 2 + 1):
+        moving = lax.ppermute(moving, "row", onward)
+        pairs.append(moving)
+        if hop < chips // 2:
+            pairs.append(lax.ppermute(moving, "row", other_core))
+    return pairs, row_tile, col_tile
+
+
 def on_device(factor, damping):
     row = lax.axis_index("row")
     col = lax.axis_index("col")
     own = factor.reshape(FLAT, LANES)
-
-    piece = jnp.where(row == 0, own[:PIECE], 0.0)
-    arrived = [
-        lax.ppermute(own[PIECE * r:PIECE * (r + 1)], "row", [(0, r)]) for r in range(1, GRID)
-    ]
-    for other in arrived:
-        piece = piece + other
-
-    first = jnp.where(col == 0, piece, 0.0)
-    for hop in (8, 4, 2, 1):
-        pairs = [(c, c + hop) for c in range(0, GRID, 2 * hop)]
-        first = first + lax.ppermute(first, "col", pairs)
-
-    swap = [(r * GRID + c, c * GRID + r) for r in range(GRID) for c in range(GRID)]
-    turned = lax.ppermute(piece, ("row", "col"), swap)
-
-    col_tile = lax.all_gather(piece, "row", axis=0, tiled=True)
-    first_tile = lax.all_gather(first, "row", axis=0, tiled=True)
-    row_tile = lax.all_gather(turned, "col", axis=0, tiled=True)
-
-    high, low, upper = factorize(damping, first_tile)
+    pairs, row_tile, col_tile = spread(own)
     where = jnp.stack([row, col]).astype(jnp.int32)
+    high, low, upper = factorize(where, damping, pairs)
     result = finish(where, damping, high, low, upper, row_tile, col_tile, own)
     return result.reshape(factor.shape)
 

time: 244 us -> 213 us (0.87)
  waiting for transfers between devices: 128 us -> 74.3 us
  starting transfers between devices: 18.3 us -> 39.1 us
    all_gather x3 -> x2, waiting for transfers between devices: 111 us -> 0.01 us  [the longest x1 0.01 us: spread(): row_tile = lax.all_gather(turned, 'col', axis=0, tiled=True)]
    ppermute x20 -> x28, waiting for transfers between devices: 16.4 us -> 74.3 us  [the longest x4 53.7 us: spread(): first = first + lax.ppermute(first, 'col', pairs)]
    ppermute x20 -> x28, starting transfers between devices: 18.3 us -> 39 us  [the longest x15 13.4 us: spread(): lax.ppermute(own[size * r:size * (r + 1)], 'row', [(0, r)])]
  transfers between devices with their start and end apart: 23 -> 30, of which waited for: 3 -> 6; matrix products, arithmetic and copies ran while one was open for 0% -> 0% of each run, Pallas kernels for 22% -> 25%
where the time goes in v2:
time: 213 us; the launch traced here: 211 us
  Pallas kernels  74.6 us (35%)
  waiting for transfers between devices  74.3 us (35%)
  starting transfers between devices  39.1 us (18%)
  between operations  14.4 us (7%)
  other arithmetic  7.09 us (3%)
    ppermute x4, waiting for transfers between devices, spread(): first = first + lax.ppermute(first, 'col', pairs)  53.7 us
    pallas_call x1, Pallas kernels, factorize(): pl.pallas_call(factor_kernel, out_shape=[jax.ShapeDtypeStruct((ORDER, ORD...  53.7 us
    pallas_call x1, Pallas kernels, finish(): pl.pallas_call(update_kernel, out_shape=jax.ShapeDtypeStruct((FLAT, LANES...  20.9 us
    ppermute x4, waiting for transfers between devices, spread(): moving = lax.ppermute(moving, 'row', onward)  19.4 us
    ppermute x15, starting transfers between devices, spread(): lax.ppermute(own[size * r:size * (r + 1)], 'row', [(0, r)])  13.4 us
    ppermute x4, starting transfers between devices, spread(): moving = lax.ppermute(moving, 'row', onward)  11.8 us
    ppermute x3, starting transfers between devices, spread(): pairs.append(lax.ppermute(moving, 'row', other_core))  4.66 us
  transfers between devices with their start and end apart: 30, of which 6 were waited for; matrix products, arithmetic and copies ran while one was open for 0% of the time, Pallas kernels for 25%

profile of v2, /device:TPU:9, one launch (start us, length us, event | category | flops | bytes accessed | tf_op | source)
XLA Modules:
  0.0 210.9 jit_solution(3397772766326872730)
XLA Ops:
  6.5 4.1 %fusion = (f32[1,1,56,1,1,896]{5,4,3,2,1,0:T(1,128)S(1)}, f32[1,1,56,1,1,896]{5,4,3,2,1,0:T(1,128)S(1)}, f32[1,1,56,1,1,896]{5,4,3,2,1,0:T(1,128)S(1)}, f32[1,1,...) fusion(f32[1,1,896,1,1,896]{5,4,3,2,1,0:T(1,128)} %param.2, ...), kind=kLoop, calls=%fused_computation.7 | loop fusion | flops 50176 | bytes 6422529 | tf_op jit(solution)/shard_map/slice | solution.py:235
  10.6 1.3 collective-permute-start
  11.9 0.7 collective-permute-start.1
  12.6 0.7 collective-permute-start.10
  13.3 0.7 collective-permute-start.11
  14.0 0.7 collective-permute-start.12
  14.7 0.7 collective-permute-start.13
  15.3 0.7 collective-permute-start.14
  16.0 0.7 collective-permute-start.2
  16.7 0.7 collective-permute-start.3
  18.8 1.4 collective-permute-start.6
  20.2 1.3 collective-permute-start.7
  21.5 1.3 collective-permute-start.8
  22.8 1.3 collective-permute-start.9
  24.2 2.2 %broadcast_select_fusion.1 = (f32[392,128]{1,0:T(8,128)S(1)}, f32[392,128]{1,0:T(8,128)}) fusion(pred[]{:T(512)S(6)} %eq.13, f32[392,128]{1,0:T(8,128)S(1)} %collective-permute-done.14, f32[392,128]{1,0:T(8,128)S(1)} %collective-permute-done.13, f32[392,128]{1,0:T(8,128)S(1)} %collective-permute-done.12, f32[392,128]{1,0:T(8,128)S(1)} %collective-permute-done.11, ...), kind=kLoop, calls=%fused_computation.3 | loop fusion | flops 802816 | bytes 3612673 | tf_op jit(solution)/shard_map/jit(_where)/select_n | solution.py:245
  26.4 1.6 collective-permute-start.27
  28.0 0.7 copy-done.8
  30.9 1.3 collective-permute-start.18
  32.2 53.7 %collective-permute-done.18 = f32[392,128]{1,0:T(8,128)S(1)} collective-permute-done((f32[392,128]{1,0:T(8,128)S(1)}, f32[392,128]{1,0:T(8,128)S(1)}, u32[]{:S(2)}, u32[]{:S(2)}) %collective-permute-start.18) | collective-permute-done | bytes 200736 | tf_op jit(solution)/shard_map/ppermute | solution.py:248
  86.0 4.2 %collective-permute-start.19 = (f32[392,128]{1,0:T(8,128)S(1)}, f32[392,128]{1,0:T(8,128)S(1)}, u32[]{:S(2)}, u32[]{:S(2)}) collective-permute-start(f32[392,128]{1,0:T(8,128)S(1)} %add.80), channel_id=1, source_target_pairs={{0,16},{16,0},{32,48},{48,32},{64,80},{80,64},{96,112},{112,96},{1... | collective-permute-start | bytes 602120 | tf_op jit(solution)/shard_map/ppermute | solution.py:254
  90.2 1.1 collective-permute-done.19
  91.4 4.4 %collective-permute-start.20 = (f32[784,128]{1,0:T(8,128)S(1)}, f32[784,128]{1,0:T(8,128)S(1)}, u32[]{:S(2)}, u32[]{:S(2)}) collective-permute-start(f32[784,128]{1,0:T(8,128)S(1)} %pad_maximum_fusion.refs_0_), channel_id=1, source_target_pairs={{0,32},{32,64},{64,96},{96,128},{128,160},{160,192},{192,224},{224... | collective-permute-start | bytes 1204232 | tf_op jit(solution)/shard_map/ppermute | solution.py:260
  95.8 5.2 %collective-permute-done.20.refs_1_ = f32[784,128]{1,0:T(8,128)S(1)} collective-permute-done((f32[784,128]{1,0:T(8,128)S(1)}, f32[784,128]{1,0:T(8,128)S(1)}, u32[]{:S(2)}, u32[]{:S(2)}) %collective-permute-start.20) | collective-permute-done | bytes 401440 | tf_op jit(solution)/shard_map/ppermute | solution.py:260
  101.0 3.8 %collective-permute-start.22 = (f32[784,128]{1,0:T(8,128)S(1)}, f32[784,128]{1,0:T(8,128)S(1)}, u32[]{:S(2)}, u32[]{:S(2)}) collective-permute-start(f32[784,128]{1,0:T(8,128)S(1)} %collective-permute-done.20.refs_1_), channel_id=1, source_target_pairs={{0,32},{32,64},{64,96},{96,128},{128,160},{160,192},{192,224},{224... | collective-permute-start | bytes 1204232 | tf_op jit(solution)/shard_map/ppermute | solution.py:260
  104.8 4.8 %collective-permute-done.22.refs_3_ = f32[784,128]{1,0:T(8,128)S(1)} collective-permute-done((f32[784,128]{1,0:T(8,128)S(1)}, f32[784,128]{1,0:T(8,128)S(1)}, u32[]{:S(2)}, u32[]{:S(2)}) %collective-permute-start.22) | collective-permute-done | bytes 401440 | tf_op jit(solution)/shard_map/ppermute | solution.py:260
  109.6 3.1 %collective-permute-start.24 = (f32[784,128]{1,0:T(8,128)S(1)}, f32[784,128]{1,0:T(8,128)S(1)}, u32[]{:S(2)}, u32[]{:S(2)}) collective-permute-start(f32[784,128]{1,0:T(8,128)S(1)} %collective-permute-done.22.refs_3_), channel_id=1, source_target_pairs={{0,32},{32,64},{64,96},{96,128},{128,160},{160,192},{192,224},{224... | collective-permute-start | bytes 1204232 | tf_op jit(solution)/shard_map/ppermute | solution.py:260
  113.2 4.3 %collective-permute-done.24.refs_5_ = f32[784,128]{1,0:T(8,128)S(1)} collective-permute-done((f32[784,128]{1,0:T(8,128)S(1)}, f32[784,128]{1,0:T(8,128)S(1)}, u32[]{:S(2)}, u32[]{:S(2)}) %collective-permute-start.24) | collective-permute-done | bytes 401440 | tf_op jit(solution)/shard_map/ppermute | solution.py:260
  117.5 4.1 %collective-permute-start.25 = (f32[784,128]{1,0:T(8,128)S(1)}, f32[784,128]{1,0:T(8,128)S(1)}, u32[]{:S(2)}, u32[]{:S(2)}) collective-permute-start(f32[784,128]{1,0:T(8,128)S(1)} %collective-permute-done.24.refs_5_), channel_id=1, source_target_pairs={{0,16},{16,0},{32,48},{48,32},{64,80},{80,64},{96,112},{112,96},{1... | collective-permute-start | bytes 1204232 | tf_op jit(solution)/shard_map/ppermute | solution.py:263
  123.6 5.1 %collective-permute-done.26.refs_7_ = f32[784,128]{1,0:T(8,128)S(1)} collective-permute-done((f32[784,128]{1,0:T(8,128)S(1)}, f32[784,128]{1,0:T(8,128)S(1)}, u32[]{:S(2)}, u32[]{:S(2)}) %collective-permute-start.26) | collective-permute-done | bytes 401440 | tf_op jit(solution)/shard_map/ppermute | solution.py:260
  128.7 0.8 copy-done.7
  129.5 53.7 %factorize.1 = (bf16[896,896]{1,0:T(8,128)(2,1)}, bf16[896,896]{1,0:T(8,128)(2,1)}, f32[896,896]{1,0:T(8,128)}) custom-call(s32[2]{0:T(128)} %pad_add_fusion.where_ref, f32[1]{0:T(128)S(6)} %copy.4.damping_ref, f32[784,128]{1,0:T(8,128)} %copy-done, f32[784,128]{1,0:T(8,128)} %copy-done.1, f32[784,128]{1,0:T(8,128)} %copy-done.4, f32[784,128]{1,0:T(8,128)} %copy-done.2, ...), custom_call_target="tpu_custom_call" | custom-call | tf_op jit(solution)/shard_map/factorize/pallas_call | solution.py:200
  183.2 20.9 %finish.1 = f32[6272,128]{1,0:T(8,128)} custom-call(s32[2]{0:T(128)} %pad_add_fusion.where_ref, f32[1]{0:T(128)S(6)} %copy.4.damping_ref, bf16[896,896]{1,0:T(8,128)(2,1)} %get-tuple-element.8.high_ref, bf16[896,896]{1,0:T(8,128)(2,1)} %get-tuple-element.9.low_ref, f32[896,896]{1,0:T(8,128)} %get-tuple-element.10.upper_ref, ...), custom_call_target="tpu_custom_call" | custom-call | tf_op jit(solution)/shard_map/finish/pallas_call | solution.py:216
  (59 shorter events, 5.5 us)
Async XLA Ops:
  6.5 176.7 %all-gather.5.cloned.1.call-start = ((), (), s32[]{:S(2)}) async-start(), calls=%async_computation.1 | async-start | bytes 3411968 | tf_op jit(solution)/shard_map/all_gather | solution.py:243
  10.6 4.0 %collective-permute-start = (f32[392,128]{1,0:T(8,128)S(1)}, f32[392,128]{1,0:T(8,128)S(1)}, u32[]{:S(2)}, u32[]{:S(2)}) collective-permute-start(f32[392,128]{1,0:T(8,128)S(1)} %bitcast.36), channel_id=1, source_target_pairs={{0,16},{1,17},{2,18},{3,19},{4,20},{5,21},{6,22},{7,23},{8,24},{9,... | collective-permute-start | bytes 602120 | tf_op jit(solution)/shard_map/ppermute | solution.py:235
  11.9 3.4 %collective-permute-start.1 = (f32[392,128]{1,0:T(8,128)S(1)}, f32[392,128]{1,0:T(8,128)S(1)}, u32[]{:S(2)}, u32[]{:S(2)}) collective-permute-start(f32[392,128]{1,0:T(8,128)S(1)} %bitcast.35), channel_id=1, source_target_pairs={{0,32},{1,33},{2,34},{3,35},{4,36},{5,37},{6,38},{7,39},{8,40},{9,... | collective-permute-start | bytes 602120 | tf_op jit(solution)/shard_map/ppermute | solution.py:235
  12.6 3.4 %collective-permute-start.10 = (f32[392,128]{1,0:T(8,128)S(1)}, f32[392,128]{1,0:T(8,128)S(1)}, u32[]{:S(2)}, u32[]{:S(2)}) collective-permute-start(f32[392,128]{1,0:T(8,128)S(1)} %bitcast.34), channel_id=1, source_target_pairs={{0,176},{1,177},{2,178},{3,179},{4,180},{5,181},{6,182},{7,183},{8... | collective-permute-start | bytes 602120 | tf_op jit(solution)/shard_map/ppermute | solution.py:235
  13.3 3.4 %collective-permute-start.11 = (f32[392,128]{1,0:T(8,128)S(1)}, f32[392,128]{1,0:T(8,128)S(1)}, u32[]{:S(2)}, u32[]{:S(2)}) collective-permute-start(f32[392,128]{1,0:T(8,128)S(1)} %bitcast.33), channel_id=1, source_target_pairs={{0,192},{1,193},{2,194},{3,195},{4,196},{5,197},{6,198},{7,199},{8... | collective-permute-start | bytes 602120 | tf_op jit(solution)/shard_map/ppermute | solution.py:235
  14.0 3.5 %collective-permute-start.12 = (f32[392,128]{1,0:T(8,128)S(1)}, f32[392,128]{1,0:T(8,128)S(1)}, u32[]{:S(2)}, u32[]{:S(2)}) collective-permute-start(f32[392,128]{1,0:T(8,128)S(1)} %bitcast.32), channel_id=1, source_target_pairs={{0,208},{1,209},{2,210},{3,211},{4,212},{5,213},{6,214},{7,215},{8... | collective-permute-start | bytes 602120 | tf_op jit(solution)/shard_map/ppermute | solution.py:235
  14.7 3.5 %collective-permute-start.13 = (f32[392,128]{1,0:T(8,128)S(1)}, f32[392,128]{1,0:T(8,128)S(1)}, u32[]{:S(2)}, u32[]{:S(2)}) collective-permute-start(f32[392,128]{1,0:T(8,128)S(1)} %bitcast.31), channel_id=1, source_target_pairs={{0,224},{1,225},{2,226},{3,227},{4,228},{5,229},{6,230},{7,231},{8... | collective-permute-start | bytes 602120 | tf_op jit(solution)/shard_map/ppermute | solution.py:235
  15.3 3.5 %collective-permute-start.14 = (f32[392,128]{1,0:T(8,128)S(1)}, f32[392,128]{1,0:T(8,128)S(1)}, u32[]{:S(2)}, u32[]{:S(2)}) collective-permute-start(f32[392,128]{1,0:T(8,128)S(1)} %bitcast.30), channel_id=1, source_target_pairs={{0,240},{1,241},{2,242},{3,243},{4,244},{5,245},{6,246},{7,247},{8... | collective-permute-start | bytes 602120 | tf_op jit(solution)/shard_map/ppermute | solution.py:235
  16.0 4.1 %collective-permute-start.2 = (f32[392,128]{1,0:T(8,128)S(1)}, f32[392,128]{1,0:T(8,128)S(1)}, u32[]{:S(2)}, u32[]{:S(2)}) collective-permute-start(f32[392,128]{1,0:T(8,128)S(1)} %bitcast.29), channel_id=1, source_target_pairs={{0,48},{1,49},{2,50},{3,51},{4,52},{5,53},{6,54},{7,55},{8,56},{9,... | collective-permute-start | bytes 602120 | tf_op jit(solution)/shard_map/ppermute | solution.py:235
  16.7 4.8 %collective-permute-start.3 = (f32[392,128]{1,0:T(8,128)S(1)}, f32[392,128]{1,0:T(8,128)S(1)}, u32[]{:S(2)}, u32[]{:S(2)}) collective-permute-start(f32[392,128]{1,0:T(8,128)S(1)} %bitcast.28), channel_id=1, source_target_pairs={{0,64},{1,65},{2,66},{3,67},{4,68},{5,69},{6,70},{7,71},{8,72},{9,... | collective-permute-start | bytes 602120 | tf_op jit(solution)/shard_map/ppermute | solution.py:235
  17.4 5.4 %collective-permute-start.4 = (f32[392,128]{1,0:T(8,128)S(1)}, f32[392,128]{1,0:T(8,128)S(1)}, u32[]{:S(2)}, u32[]{:S(2)}) collective-permute-start(f32[392,128]{1,0:T(8,128)S(1)} %bitcast.27), channel_id=1, source_target_pairs={{0,80},{1,81},{2,82},{3,83},{4,84},{5,85},{6,86},{7,87},{8,88},{9,... | collective-permute-start | bytes 602120 | tf_op jit(solution)/shard_map/ppermute | solution.py:235
  18.1 6.1 %collective-permute-start.5 = (f32[392,128]{1,0:T(8,128)S(1)}, f32[392,128]{1,0:T(8,128)S(1)}, u32[]{:S(2)}, u32[]{:S(2)}) collective-permute-start(f32[392,128]{1,0:T(8,128)S(1)} %bitcast.26), channel_id=1, source_target_pairs={{0,96},{1,97},{2,98},{3,99},{4,100},{5,101},{6,102},{7,103},{8,104... | collective-permute-start | bytes 602120 | tf_op jit(solution)/shard_map/ppermute | solution.py:235
  18.8 5.4 %collective-permute-start.6 = (f32[392,128]{1,0:T(8,128)S(1)}, f32[392,128]{1,0:T(8,128)}, u32[]{:S(2)}, u32[]{:S(2)}) collective-permute-start(f32[392,128]{1,0:T(8,128)S(1)} %bitcast.25), channel_id=1, source_target_pairs={{0,112},{1,113},{2,114},{3,115},{4,116},{5,117},{6,118},{7,119},{8... | collective-permute-start | bytes 602120 | tf_op jit(solution)/shard_map/ppermute | solution.py:235
  20.2 4.0 %collective-permute-start.7 = (f32[392,128]{1,0:T(8,128)S(1)}, f32[392,128]{1,0:T(8,128)}, u32[]{:S(2)}, u32[]{:S(2)}) collective-permute-start(f32[392,128]{1,0:T(8,128)S(1)} %bitcast.24), channel_id=1, source_target_pairs={{0,128},{1,129},{2,130},{3,131},{4,132},{5,133},{6,134},{7,135},{8... | collective-permute-start | bytes 602120 | tf_op jit(solution)/shard_map/ppermute | solution.py:235
  21.5 2.7 %collective-permute-start.8 = (f32[392,128]{1,0:T(8,128)S(1)}, f32[392,128]{1,0:T(8,128)}, u32[]{:S(2)}, u32[]{:S(2)}) collective-permute-start(f32[392,128]{1,0:T(8,128)S(1)} %bitcast.23), channel_id=1, source_target_pairs={{0,144},{1,145},{2,146},{3,147},{4,148},{5,149},{6,150},{7,151},{8... | collective-permute-start | bytes 602120 | tf_op jit(solution)/shard_map/ppermute | solution.py:235
  22.8 1.4 collective-permute-start.9
  26.4 156.8 %all-gather.3.cloned.1.call-start = ((), (), s32[]{:S(2)}) async-start(), calls=%async_computation | async-start | bytes 3411968 | tf_op jit(solution)/shard_map/all_gather | solution.py:242
  26.4 1.6 collective-permute-start.27
  28.7 0.7 collective-permute-start.15
  29.5 0.7 collective-permute-start.16
  30.2 0.7 collective-permute-start.17
  30.9 55.0 %collective-permute-start.18 = (f32[392,128]{1,0:T(8,128)S(1)}, f32[392,128]{1,0:T(8,128)S(1)}, u32[]{:S(2)}, u32[]{:S(2)}) collective-permute-start(f32[392,128]{1,0:T(8,128)S(1)} %add.79), channel_id=1, source_target_pairs={{0,1},{2,3},{4,5},{6,7},{8,9},{10,11},{12,13},{14,15},{16,17},{18,... | collective-permute-start | bytes 602120 | tf_op jit(solution)/shard_map/ppermute | solution.py:248
  86.0 5.3 %collective-permute-start.19 = (f32[392,128]{1,0:T(8,128)S(1)}, f32[392,128]{1,0:T(8,128)S(1)}, u32[]{:S(2)}, u32[]{:S(2)}) collective-permute-start(f32[392,128]{1,0:T(8,128)S(1)} %add.80), channel_id=1, source_target_pairs={{0,16},{16,0},{32,48},{48,32},{64,80},{80,64},{96,112},{112,96},{1... | collective-permute-start | bytes 602120 | tf_op jit(solution)/shard_map/ppermute | solution.py:254
  91.4 37.3 %copy-start = (f32[784,128]{1,0:T(8,128)}, f32[784,128]{1,0:T(8,128)S(1)}, u32[]{:S(2)}) copy-start(f32[784,128]{1,0:T(8,128)S(1)} %pad_maximum_fusion.refs_0_) | copy-start | bytes 1204228
  91.4 9.6 %collective-permute-start.20 = (f32[784,128]{1,0:T(8,128)S(1)}, f32[784,128]{1,0:T(8,128)S(1)}, u32[]{:S(2)}, u32[]{:S(2)}) collective-permute-start(f32[784,128]{1,0:T(8,128)S(1)} %pad_maximum_fusion.refs_0_), channel_id=1, source_target_pairs={{0,32},{32,64},{64,96},{96,128},{128,160},{160,192},{192,224},{224... | collective-permute-start | bytes 1204232 | tf_op jit(solution)/shard_map/ppermute | solution.py:260
  101.0 27.7 %copy-start.1 = (f32[784,128]{1,0:T(8,128)}, f32[784,128]{1,0:T(8,128)S(1)}, u32[]{:S(2)}) copy-start(f32[784,128]{1,0:T(8,128)S(1)} %collective-permute-done.20.refs_1_) | copy-start | bytes 1204228
  101.0 8.6 %collective-permute-start.22 = (f32[784,128]{1,0:T(8,128)S(1)}, f32[784,128]{1,0:T(8,128)S(1)}, u32[]{:S(2)}, u32[]{:S(2)}) collective-permute-start(f32[784,128]{1,0:T(8,128)S(1)} %collective-permute-done.20.refs_1_), channel_id=1, source_target_pairs={{0,32},{32,64},{64,96},{96,128},{128,160},{160,192},{192,224},{224... | collective-permute-start | bytes 1204232 | tf_op jit(solution)/shard_map/ppermute | solution.py:260
  109.6 7.9 %collective-permute-start.24 = (f32[784,128]{1,0:T(8,128)S(1)}, f32[784,128]{1,0:T(8,128)S(1)}, u32[]{:S(2)}, u32[]{:S(2)}) collective-permute-start(f32[784,128]{1,0:T(8,128)S(1)} %collective-permute-done.22.refs_3_), channel_id=1, source_target_pairs={{0,32},{32,64},{64,96},{96,128},{128,160},{160,192},{192,224},{224... | collective-permute-start | bytes 1204232 | tf_op jit(solution)/shard_map/ppermute | solution.py:260
  112.7 10.8 %collective-permute-start.21 = (f32[784,128]{1,0:T(8,128)S(1)}, f32[784,128]{1,0:T(8,128)S(1)}, u32[]{:S(2)}, u32[]{:S(2)}) collective-permute-start(f32[784,128]{1,0:T(8,128)S(1)} %collective-permute-done.20.refs_1_), channel_id=1, source_target_pairs={{0,16},{16,0},{32,48},{48,32},{64,80},{80,64},{96,112},{112,96},{1... | collective-permute-start | bytes 1204232 | tf_op jit(solution)/shard_map/ppermute | solution.py:263
  112.7 10.8 %collective-permute-start.23 = (f32[784,128]{1,0:T(8,128)S(1)}, f32[784,128]{1,0:T(8,128)S(1)}, u32[]{:S(2)}, u32[]{:S(2)}) collective-permute-start(f32[784,128]{1,0:T(8,128)S(1)} %collective-permute-done.22.refs_3_), channel_id=1, source_target_pairs={{0,16},{16,0},{32,48},{48,32},{64,80},{80,64},{96,112},{112,96},{1... | collective-permute-start | bytes 1204232 | tf_op jit(solution)/shard_map/ppermute | solution.py:263
  117.5 6.0 %collective-permute-start.25 = (f32[784,128]{1,0:T(8,128)S(1)}, f32[784,128]{1,0:T(8,128)S(1)}, u32[]{:S(2)}, u32[]{:S(2)}) collective-permute-start(f32[784,128]{1,0:T(8,128)S(1)} %collective-permute-done.24.refs_5_), channel_id=1, source_target_pairs={{0,16},{16,0},{32,48},{48,32},{64,80},{80,64},{96,112},{112,96},{1... | collective-permute-start | bytes 1204232 | tf_op jit(solution)/shard_map/ppermute | solution.py:263
  121.7 7.0 %collective-permute-start.26 = (f32[784,128]{1,0:T(8,128)S(1)}, f32[784,128]{1,0:T(8,128)S(1)}, u32[]{:S(2)}, u32[]{:S(2)}) collective-permute-start(f32[784,128]{1,0:T(8,128)S(1)} %collective-permute-done.24.refs_5_), channel_id=1, source_target_pairs={{0,32},{32,64},{64,96},{96,128},{128,160},{160,192},{192,224},{224... | collective-permute-start | bytes 1204232 | tf_op jit(solution)/shard_map/ppermute | solution.py:260
  (7 other events, 47.3 us)
Sparse Core Ops, SparseCore 0:
  26.5 69.5 all-gather.4
  98.6 49.3 all-gather.2

commit v3 on v2

--- a/solution.py
+++ b/solution.py
@@ -4,6 +4,7 @@
 from jax.experimental import pallas as pl
 from jax.experimental.pallas import tpu as pltpu
 from jax.sharding import PartitionSpec as P
+
 
 F32 = jnp.float32
 BF16 = jnp.bfloat16
@@ -15,6 +16,7 @@
 CHIPS = GRID // 2
 PAIR_ROWS = ORDER // CHIPS
 GROUPS = ((0, 256), (256, 512), (512, 768), (768, 896))
+SCATTER = (4, 3, 5, 2, 6, 1, 7)
 INTERPRET = False
 
 
@@ -228,39 +230,42 @@
     row = lax.axis_index("row")
     col = lax.axis_index("col")
     core = row % 2
-    size = own.shape[0] // GRID
+    chips = GRID // 2
+    size = own.shape[0] // chips
 
     piece = jnp.where(row == 0, own[:size], 0.0)
     arrived = [
-        lax.ppermute(own[size * r:size * (r + 1)], "row", [(0, r)]) for r in range(1, GRID)
+        lax.ppermute(own[size * z:size * (z + 1)], "row", [(0, 2 * z)]) for z in SCATTER
     ]
     for other in arrived:
         piece = piece + other
 
+    second = lax.ppermute(piece[size // 2:], "row", [(2 * z, 2 * z + 1) for z in range(chips)])
+    half = jnp.where(core == 0, piece[:size // 2], second)
+    col_tile = lax.all_gather(half, "row", axis=0, tiled=True)
     swap = [(r * GRID + c, c * GRID + r) for r in range(GRID) for c in range(GRID)]
-    turned = lax.ppermute(piece, ("row", "col"), swap)
-    row_tile = lax.all_gather(turned, "col", axis=0, tiled=True)
-    col_tile = lax.all_gather(piece, "row", axis=0, tiled=True)
-
-    first = jnp.where(col == 0, piece, 0.0)
+    turned = lax.ppermute(half, ("row", "col"), swap)
+
+    moving = jnp.where(col == 0, piece, 0.0)
     for hop in (8, 4, 2, 1):
-        pairs = [(c, c + hop) for c in range(0, GRID, 2 * hop)]
-        first = first + lax.ppermute(first, "col", pairs)
-
-    chips = GRID // 2
+        moving = moving + lax.ppermute(
+            moving, ("row", "col"),
+            [(2 * z * GRID + c, 2 * z * GRID + c + hop) for z in range(chips) for c in range(0, GRID, 2 * hop)],
+        )
+    moving = moving + lax.ppermute(moving, "row", [(2 * z, 2 * z + 1) for z in range(chips)])
+
     other_core = [(r, r ^ 1) for r in range(GRID)]
     onward = [(2 * z, 2 * ((z + 1) % chips)) for z in range(chips)]
     onward += [(2 * z + 1, 2 * ((z - 1) % chips) + 1) for z in range(chips)]
-    partner = lax.ppermute(first, "row", other_core)
-    moving = jnp.concatenate(
-        [jnp.where(core == 0, first, partner), jnp.where(core == 0, partner, first)], axis=0
-    )
     pairs = [moving]
     for hop in range(1, chips // 2 + 1):
         moving = lax.ppermute(moving, "row", onward)
+        if hop == 3:
+            moving, turned = lax.optimization_barrier((moving, turned))
         pairs.append(moving)
         if hop < chips // 2:
             pairs.append(lax.ppermute(moving, "row", other_core))
+    row_tile = lax.all_gather(turned, "col", axis=0, tiled=True)
     return pairs, row_tile, col_tile
 
 

time: 213 us -> 217 us (1.019)
  starting transfers between devices: 39.1 us -> 49.6 us
  waiting for transfers between devices: 74.3 us -> 69.9 us
    ppermute x4, starting transfers between devices: 11.8 us -> 31.3 us  [spread(): moving = lax.ppermute(moving, 'row', onward)]
    ppermute x21 -> x14, starting transfers between devices: 22.5 us -> 13.1 us  [the longest x7 6.99 us: spread(): lax.ppermute(own[size * z:size * (z + 1)], 'row', [(0, 2 * z)])]
    ppermute x21 -> x14, waiting for transfers between devices: 54.9 us -> 51.6 us  [the longest x1 29.7 us: spread(): lax.ppermute(moving, 'row', [(2 * z, 2 * z + 1) for z in range(chips)])]
  transfers between devices with their start and end apart: 30 -> 23, of which waited for: 6 -> 6; matrix products, arithmetic and copies ran while one was open for 0% -> 0% of each run, Pallas kernels for 25% -> 25%
where the time goes in v3:
time: 217 us
  Pallas kernels  74.6 us (34%)
  waiting for transfers between devices  69.9 us (32%)
  starting transfers between devices  49.6 us (23%)
  between operations  14.3 us (7%)
  other arithmetic  7.7 us (4%)
    pallas_call x1, Pallas kernels, factorize(): pl.pallas_call(factor_kernel, out_shape=[jax.ShapeDtypeStruct((ORDER, ORD...  53.7 us
    ppermute x4, starting transfers between devices, spread(): moving = lax.ppermute(moving, 'row', onward)  31.3 us
    ppermute x1, waiting for transfers between devices, spread(): lax.ppermute(moving, 'row', [(2 * z, 2 * z + 1) for z in range(chips)])  29.7 us
    ppermute x1, waiting for transfers between devices, spread(): lax.ppermute(piece[size // 2:], 'row', [(2 * z, 2 * z + 1) for z in range...  21.9 us
    pallas_call x1, Pallas kernels, finish(): pl.pallas_call(update_kernel, out_shape=jax.ShapeDtypeStruct((FLAT, LANES...  20.9 us
    ppermute x4, waiting for transfers between devices, spread(): moving = lax.ppermute(moving, 'row', onward)  18.2 us
    ppermute x7, starting transfers between devices, spread(): lax.ppermute(own[size * z:size * (z + 1)], 'row', [(0, 2 * z)])  6.99 us
    ppermute x3, starting transfers between devices, spread(): pairs.append(lax.ppermute(moving, 'row', other_core))  5.22 us
  transfers between devices with their start and end apart: 23, of which 6 were waited for; matrix products, arithmetic and copies ran while one was open for 0% of the time, Pallas kernels for 25%

profile of v3, /device:TPU:9, one launch (start us, length us, event | category | flops | bytes accessed | tf_op | source)
XLA Modules:
  0.0 216.9 jit_solution(12916477119734052845)
XLA Ops:
  6.5 4.6 %fusion = (f32[1,1,112,1,1,896]{5,4,3,2,1,0:T(1,128)S(1)}, f32[1,1,112,1,1,896]{5,4,3,2,1,0:T(1,128)S(1)}, f32[1,1,112,1,1,896]{5,4,3,2,1,0:T(1,128)S(1)}, f32[1...) fusion(f32[1,1,896,1,1,896]{5,4,3,2,1,0:T(1,128)} %param.2, ...), kind=kLoop, calls=%fused_computation.5 | loop fusion | flops 100352 | bytes 6422529 | tf_op jit(solution)/shard_map/slice | solution.py:238
  11.1 0.7 collective-permute-start
  11.8 0.7 collective-permute-start.1
  12.5 0.7 collective-permute-start.2
  13.2 0.7 collective-permute-start.3
  13.9 1.4 collective-permute-start.4
  15.3 1.4 collective-permute-start.5
  16.7 1.4 collective-permute-start.6
  18.2 1.5 broadcast_select_fusion.1
  19.7 1.3 collective-permute-start.17
  21.0 21.9 %collective-permute-done.17 = f32[392,128]{1,0:T(8,128)S(1)} collective-permute-done((f32[392,128]{1,0:T(8,128)S(1)}, f32[392,128]{1,0:T(8,128)S(1)}, u32[]{:S(2)}, u32[]{:S(2)}) %collective-permute-start.17) | collective-permute-done | bytes 200736 | tf_op jit(solution)/shard_map/ppermute | solution.py:243
  42.9 0.7 slice_select_fusion
  43.7 0.8 collective-permute-start.7
  44.6 0.7 collective-permute-start.8
  45.3 0.7 collective-permute-start.9
  46.1 0.7 collective-permute-start.10
  46.8 1.3 collective-permute-start.11
  48.1 29.7 %collective-permute-done.11 = f32[784,128]{1,0:T(8,128)S(1)} collective-permute-done((f32[784,128]{1,0:T(8,128)S(1)}, f32[784,128]{1,0:T(8,128)S(1)}, u32[]{:S(2)}, u32[]{:S(2)}) %collective-permute-start.11) | collective-permute-done | bytes 401440 | tf_op jit(solution)/shard_map/ppermute | solution.py:255
  77.9 2.2 collective-permute-start.12
  80.1 5.8 %collective-permute-done.12.refs_1_ = f32[784,128]{1,0:T(8,128)S(1)} collective-permute-done((f32[784,128]{1,0:T(8,128)S(1)}, f32[784,128]{1,0:T(8,128)S(1)}, u32[]{:S(2)}, u32[]{:S(2)}) %collective-permute-start.12) | collective-permute-done | bytes 401440 | tf_op jit(solution)/shard_map/ppermute | solution.py:262
  85.8 2.2 collective-permute-start.14
  88.0 4.8 %collective-permute-done.14.refs_3_ = f32[784,128]{1,0:T(8,128)S(1)} collective-permute-done((f32[784,128]{1,0:T(8,128)S(1)}, f32[784,128]{1,0:T(8,128)S(1)}, u32[]{:S(2)}, u32[]{:S(2)}) %collective-permute-start.14) | collective-permute-done | bytes 401440 | tf_op jit(solution)/shard_map/ppermute | solution.py:262
  92.9 3.1 %collective-permute-start.16 = (f32[784,128]{1,0:T(8,128)S(1)}, f32[784,128]{1,0:T(8,128)S(1)}, u32[]{:S(2)}, u32[]{:S(2)}) collective-permute-start(f32[784,128]{1,0:T(8,128)S(1)} %collective-permute-done.14.refs_3_), channel_id=1, source_target_pairs={{0,32},{32,64},{64,96},{96,128},{128,160},{160,192},{192,224},{224... | collective-permute-start | bytes 1204232 | tf_op jit(solution)/shard_map/ppermute | solution.py:262
  95.9 0.7 collective-permute-start.18
  96.6 4.1 %collective-permute-done.16.refs_5_ = f32[784,128]{1,0:T(8,128)S(1)} collective-permute-done((f32[784,128]{1,0:T(8,128)S(1)}, f32[784,128]{1,0:T(8,128)S(1)}, u32[]{:S(2)}, u32[]{:S(2)}) %collective-permute-start.16) | collective-permute-done | bytes 401440 | tf_op jit(solution)/shard_map/ppermute | solution.py:262
  100.8 4.7 %collective-permute-start.13 = (f32[784,128]{1,0:T(8,128)S(1)}, f32[784,128]{1,0:T(8,128)S(1)}, u32[]{:S(2)}, u32[]{:S(2)}) collective-permute-start(f32[784,128]{1,0:T(8,128)S(1)} %collective-permute-done.12.refs_1_), channel_id=1, source_target_pairs={{0,16},{16,0},{32,48},{48,32},{64,80},{80,64},{96,112},{112,96},{1... | collective-permute-start | bytes 1204232 | tf_op jit(solution)/shard_map/ppermute | solution.py:267
  106.0 23.8 %collective-permute-start.20 = (f32[784,128]{1,0:T(8,128)S(1)}, f32[784,128]{1,0:T(8,128)S(1)}, u32[]{:S(2)}, u32[]{:S(2)}) collective-permute-start(f32[784,128]{1,0:T(8,128)S(1)} %collective-permute-done.16.refs_5_), channel_id=1, source_target_pairs={{0,32},{32,64},{64,96},{96,128},{128,160},{160,192},{192,224},{224... | collective-permute-start | bytes 1204232 | tf_op jit(solution)/shard_map/ppermute | solution.py:262
  130.5 0.7 pad_add_fusion.where_ref
  131.2 3.4 %collective-permute-done.20.refs_7_ = f32[784,128]{1,0:T(8,128)S(1)} collective-permute-done((f32[784,128]{1,0:T(8,128)S(1)}, f32[784,128]{1,0:T(8,128)S(1)}, u32[]{:S(2)}, u32[]{:S(2)}) %collective-permute-start.20) | collective-permute-done | bytes 401440 | tf_op jit(solution)/shard_map/ppermute | solution.py:262
  134.7 0.7 copy-done.8
  135.4 53.7 %factorize.1 = (bf16[896,896]{1,0:T(8,128)(2,1)}, bf16[896,896]{1,0:T(8,128)(2,1)}, f32[896,896]{1,0:T(8,128)}) custom-call(s32[2]{0:T(128)} %pad_add_fusion.where_ref, f32[1]{0:T(128)S(6)} %copy.4.damping_ref, f32[784,128]{1,0:T(8,128)} %copy-done, f32[784,128]{1,0:T(8,128)} %copy-done.2, f32[784,128]{1,0:T(8,128)} %copy-done.5, f32[784,128]{1,0:T(8,128)} %copy-done.3, ...), custom_call_target="tpu_custom_call" | custom-call | tf_op jit(solution)/shard_map/factorize/pallas_call | solution.py:202
  189.2 20.9 %finish.1 = f32[6272,128]{1,0:T(8,128)} custom-call(s32[2]{0:T(128)} %pad_add_fusion.where_ref, f32[1]{0:T(128)S(6)} %copy.4.damping_ref, bf16[896,896]{1,0:T(8,128)(2,1)} %get-tuple-element.11.high_ref, bf16[896,896]{1,0:T(8,128)(2,1)} %get-tuple-element.12.low_ref, f32[896,896]{1,0:T(8,128)} %get-tuple-element.13.upper_ref, ...), custom_call_target="tpu_custom_call" | custom-call | tf_op jit(solution)/shard_map/finish/pallas_call | solution.py:218
  (48 shorter events, 0.9 us)
Async XLA Ops:
  6.5 182.6 %all-gather.5.cloned.1.call-start = ((), (), s32[]{:S(2)}) async-start(), calls=%async_computation.1 | async-start | bytes 3411968 | tf_op jit(solution)/shard_map/all_gather | solution.py:245
  11.1 4.2 %collective-permute-start = (f32[784,128]{1,0:T(8,128)S(1)}, f32[784,128]{1,0:T(8,128)S(1)}, u32[]{:S(2)}, u32[]{:S(2)}) collective-permute-start(f32[784,128]{1,0:T(8,128)S(1)} %bitcast.18), channel_id=1, source_target_pairs={{0,128},{1,129},{2,130},{3,131},{4,132},{5,133},{6,134},{7,135},{8... | collective-permute-start | bytes 1204232 | tf_op jit(solution)/shard_map/ppermute | solution.py:238
  11.8 4.9 %collective-permute-start.1 = (f32[784,128]{1,0:T(8,128)S(1)}, f32[784,128]{1,0:T(8,128)S(1)}, u32[]{:S(2)}, u32[]{:S(2)}) collective-permute-start(f32[784,128]{1,0:T(8,128)S(1)} %bitcast.17), channel_id=1, source_target_pairs={{0,96},{1,97},{2,98},{3,99},{4,100},{5,101},{6,102},{7,103},{8,104... | collective-permute-start | bytes 1204232 | tf_op jit(solution)/shard_map/ppermute | solution.py:238
  12.5 5.7 %collective-permute-start.2 = (f32[784,128]{1,0:T(8,128)}, f32[784,128]{1,0:T(8,128)S(1)}, u32[]{:S(2)}, u32[]{:S(2)}) collective-permute-start(f32[784,128]{1,0:T(8,128)} %bitcast.5), channel_id=1, source_target_pairs={{0,160},{1,161},{2,162},{3,163},{4,164},{5,165},{6,166},{7,167},{8... | collective-permute-start | bytes 1204232 | tf_op jit(solution)/shard_map/ppermute | solution.py:238
  13.2 5.0 %collective-permute-start.3 = (f32[784,128]{1,0:T(8,128)}, f32[784,128]{1,0:T(8,128)S(1)}, u32[]{:S(2)}, u32[]{:S(2)}) collective-permute-start(f32[784,128]{1,0:T(8,128)} %bitcast.6), channel_id=1, source_target_pairs={{0,64},{1,65},{2,66},{3,67},{4,68},{5,69},{6,70},{7,71},{8,72},{9,... | collective-permute-start | bytes 1204232 | tf_op jit(solution)/shard_map/ppermute | solution.py:238
  13.9 4.3 %collective-permute-start.4 = (f32[784,128]{1,0:T(8,128)S(1)}, f32[784,128]{1,0:T(8,128)}, u32[]{:S(2)}, u32[]{:S(2)}) collective-permute-start(f32[784,128]{1,0:T(8,128)S(1)} %bitcast.16), channel_id=1, source_target_pairs={{0,192},{1,193},{2,194},{3,195},{4,196},{5,197},{6,198},{7,199},{8... | collective-permute-start | bytes 1204232 | tf_op jit(solution)/shard_map/ppermute | solution.py:238
  15.3 2.8 %collective-permute-start.5 = (f32[784,128]{1,0:T(8,128)S(1)}, f32[784,128]{1,0:T(8,128)}, u32[]{:S(2)}, u32[]{:S(2)}) collective-permute-start(f32[784,128]{1,0:T(8,128)S(1)} %bitcast.15), channel_id=1, source_target_pairs={{0,32},{1,33},{2,34},{3,35},{4,36},{5,37},{6,38},{7,39},{8,40},{9,... | collective-permute-start | bytes 1204232 | tf_op jit(solution)/shard_map/ppermute | solution.py:238
  16.7 1.4 collective-permute-start.6
  19.7 23.2 %collective-permute-start.17 = (f32[392,128]{1,0:T(8,128)S(1)}, f32[392,128]{1,0:T(8,128)S(1)}, u32[]{:S(2)}, u32[]{:S(2)}) collective-permute-start(f32[392,128]{1,0:T(8,128)S(1)} %slice.70), channel_id=1, source_target_pairs={{0,16},{32,48},{64,80},{96,112},{128,144},{160,176},{192,208},{224... | collective-permute-start | bytes 602120 | tf_op jit(solution)/shard_map/ppermute | solution.py:243
  43.6 52.4 %copy-start.1 = (f32[392,128]{1,0:T(8,128)S(1)}, f32[392,128]{1,0:T(8,128)}, u32[]{:S(2)}) copy-start(f32[392,128]{1,0:T(8,128)} %slice_select_fusion) | copy-start | bytes 602116
  43.6 145.6 %all-gather.3.cloned.1.call-start = ((), (), s32[]{:S(2)}) async-start(), calls=%async_computation | async-start | bytes 3411968 | tf_op jit(solution)/shard_map/all_gather | solution.py:268
  43.7 0.8 collective-permute-start.7
  44.6 0.7 collective-permute-start.8
  45.3 0.7 collective-permute-start.9
  46.1 0.7 collective-permute-start.10
  46.8 31.0 %collective-permute-start.11 = (f32[784,128]{1,0:T(8,128)S(1)}, f32[784,128]{1,0:T(8,128)S(1)}, u32[]{:S(2)}, u32[]{:S(2)}) collective-permute-start(f32[784,128]{1,0:T(8,128)S(1)} %add.50), channel_id=1, source_target_pairs={{0,16},{32,48},{64,80},{96,112},{128,144},{160,176},{192,208},{224... | collective-permute-start | bytes 1204232 | tf_op jit(solution)/shard_map/ppermute | solution.py:255
  77.9 56.7 %copy-start = (f32[784,128]{1,0:T(8,128)}, f32[784,128]{1,0:T(8,128)S(1)}, u32[]{:S(2)}) copy-start(f32[784,128]{1,0:T(8,128)S(1)} %add.51.refs_0_) | copy-start | bytes 1204228
  77.9 7.9 %collective-permute-start.12 = (f32[784,128]{1,0:T(8,128)S(1)}, f32[784,128]{1,0:T(8,128)S(1)}, u32[]{:S(2)}, u32[]{:S(2)}) collective-permute-start(f32[784,128]{1,0:T(8,128)S(1)} %add.51.refs_0_), channel_id=1, source_target_pairs={{0,32},{32,64},{64,96},{96,128},{128,160},{160,192},{192,224},{224... | collective-permute-start | bytes 1204232 | tf_op jit(solution)/shard_map/ppermute | solution.py:262
  85.8 48.8 %copy-start.2 = (f32[784,128]{1,0:T(8,128)}, f32[784,128]{1,0:T(8,128)S(1)}, u32[]{:S(2)}) copy-start(f32[784,128]{1,0:T(8,128)S(1)} %collective-permute-done.12.refs_1_) | copy-start | bytes 1204228
  85.8 7.0 %collective-permute-start.14 = (f32[784,128]{1,0:T(8,128)S(1)}, f32[784,128]{1,0:T(8,128)S(1)}, u32[]{:S(2)}, u32[]{:S(2)}) collective-permute-start(f32[784,128]{1,0:T(8,128)S(1)} %collective-permute-done.12.refs_1_), channel_id=1, source_target_pairs={{0,32},{32,64},{64,96},{96,128},{128,160},{160,192},{192,224},{224... | collective-permute-start | bytes 1204232 | tf_op jit(solution)/shard_map/ppermute | solution.py:262
  92.9 41.8 %copy-start.3 = (f32[784,128]{1,0:T(8,128)}, f32[784,128]{1,0:T(8,128)S(1)}, u32[]{:S(2)}) copy-start(f32[784,128]{1,0:T(8,128)S(1)} %collective-permute-done.14.refs_3_) | copy-start | bytes 1204228
  92.9 7.9 %collective-permute-start.16 = (f32[784,128]{1,0:T(8,128)S(1)}, f32[784,128]{1,0:T(8,128)S(1)}, u32[]{:S(2)}, u32[]{:S(2)}) collective-permute-start(f32[784,128]{1,0:T(8,128)S(1)} %collective-permute-done.14.refs_3_), channel_id=1, source_target_pairs={{0,32},{32,64},{64,96},{96,128},{128,160},{160,192},{192,224},{224... | collective-permute-start | bytes 1204232 | tf_op jit(solution)/shard_map/ppermute | solution.py:262
  95.9 0.7 collective-permute-start.18
  96.6 4.1 %copy-start.9 = (f32[392,128]{1,0:T(8,128)}, f32[392,128]{1,0:T(8,128)S(1)}, u32[]{:S(2)}) copy-start(f32[392,128]{1,0:T(8,128)S(1)} %collective-permute-done.18) | copy-start | bytes 602116
  100.8 33.9 %copy-start.4 = (f32[784,128]{1,0:T(8,128)}, f32[784,128]{1,0:T(8,128)S(1)}, u32[]{:S(2)}) copy-start(f32[784,128]{1,0:T(8,128)S(1)} %collective-permute-done.16.refs_5_) | copy-start | bytes 1204228
  100.8 30.4 %collective-permute-start.13 = (f32[784,128]{1,0:T(8,128)S(1)}, f32[784,128]{1,0:T(8,128)S(1)}, u32[]{:S(2)}, u32[]{:S(2)}) collective-permute-start(f32[784,128]{1,0:T(8,128)S(1)} %collective-permute-done.12.refs_1_), channel_id=1, source_target_pairs={{0,16},{16,0},{32,48},{48,32},{64,80},{80,64},{96,112},{112,96},{1... | collective-permute-start | bytes 1204232 | tf_op jit(solution)/shard_map/ppermute | solution.py:267
  105.5 25.7 %collective-permute-start.15 = (f32[784,128]{1,0:T(8,128)S(1)}, f32[784,128]{1,0:T(8,128)S(1)}, u32[]{:S(2)}, u32[]{:S(2)}) collective-permute-start(f32[784,128]{1,0:T(8,128)S(1)} %collective-permute-done.14.refs_3_), channel_id=1, source_target_pairs={{0,16},{16,0},{32,48},{48,32},{64,80},{80,64},{96,112},{112,96},{1... | collective-permute-start | bytes 1204232 | tf_op jit(solution)/shard_map/ppermute | solution.py:267
  105.6 25.6 %collective-permute-start.19 = (f32[784,128]{1,0:T(8,128)S(1)}, f32[784,128]{1,0:T(8,128)S(1)}, u32[]{:S(2)}, u32[]{:S(2)}) collective-permute-start(f32[784,128]{1,0:T(8,128)S(1)} %collective-permute-done.16.refs_5_), channel_id=1, source_target_pairs={{0,16},{16,0},{32,48},{48,32},{64,80},{80,64},{96,112},{112,96},{1... | collective-permute-start | bytes 1204232 | tf_op jit(solution)/shard_map/ppermute | solution.py:267
  106.0 28.7 %collective-permute-start.20 = (f32[784,128]{1,0:T(8,128)S(1)}, f32[784,128]{1,0:T(8,128)S(1)}, u32[]{:S(2)}, u32[]{:S(2)}) collective-permute-start(f32[784,128]{1,0:T(8,128)S(1)} %collective-permute-done.16.refs_5_), channel_id=1, source_target_pairs={{0,32},{32,64},{64,96},{96,128},{128,160},{160,192},{192,224},{224... | collective-permute-start | bytes 1204232 | tf_op jit(solution)/shard_map/ppermute | solution.py:262
  131.2 3.5 %copy-start.5 = (f32[784,128]{1,0:T(8,128)}, f32[784,128]{1,0:T(8,128)S(1)}, u32[]{:S(2)}) copy-start(f32[784,128]{1,0:T(8,128)S(1)} %collective-permute-done.13.refs_2_) | copy-start | bytes 1204228
  131.2 3.5 %copy-start.6 = (f32[784,128]{1,0:T(8,128)}, f32[784,128]{1,0:T(8,128)S(1)}, u32[]{:S(2)}) copy-start(f32[784,128]{1,0:T(8,128)S(1)} %collective-permute-done.15.refs_4_) | copy-start | bytes 1204228
  131.2 3.5 %copy-start.7 = (f32[784,128]{1,0:T(8,128)}, f32[784,128]{1,0:T(8,128)S(1)}, u32[]{:S(2)}) copy-start(f32[784,128]{1,0:T(8,128)S(1)} %collective-permute-done.19.refs_6_) | copy-start | bytes 1204228
  (1 other events, 0.7 us)
Sparse Core Ops, SparseCore 0:
  43.7 38.8 all-gather.4
  100.9 71.1 all-gather.2

commit v4 on v3

--- a/solution.py
+++ b/solution.py
@@ -14,7 +14,7 @@
 FLAT = ORDER * BLOCKS
 GRID = 16
 CHIPS = GRID // 2
-PAIR_ROWS = ORDER // CHIPS
+PIECE_ROWS = ORDER // GRID
 GROUPS = ((0, 256), (256, 512), (512, 768), (768, 896))
 SCATTER = (4, 3, 5, 2, 6, 1, 7)
 INTERPRET = False
@@ -74,30 +74,38 @@
         mixed.append(mixed_slab)
         corner.append(corner_slab)
         spread = [row_of(pivot_rows, m) for m in range(8)]
-        for other in range(slab + 1, 16):
+        for other in range(slab + 1, min(slab + 3, 16)):
             old = rows[other]
             new = jnp.where(own, 0.0, old)
             for m in range(8):
                 new = new - lane_of(old, base + m) * spread[m]
             rows[other] = new
+        far = range(slab + 3, 16)
+        if far:
+            blank = jnp.zeros((8, LANES), F32)
+            placed = jnp.concatenate([pivot_rows if i == slab else blank for i in range(16)], axis=0)
+            lanes = jnp.concatenate([jnp.where(own, rows[i], 0.0) for i in far], axis=0)
+            change = product3(split(lanes), split(placed))
+            for at, i in enumerate(far):
+                rows[i] = jnp.where(own, 0.0, rows[i]) - change[8 * at:8 * at + 8]
     return mixed, corner
 
 
 def factor_kernel(where_ref, damping_ref, *refs):
-    pair_refs, (high_ref, low_ref, upper_ref, work) = refs[:CHIPS], refs[CHIPS:]
+    piece_refs, (high_ref, low_ref, upper_ref, work) = refs[:GRID], refs[GRID:]
     damping = damping_ref[0]
     chip = where_ref[0] // 2
-    sign = 1 - 2 * (where_ref[0] % 2)
-    row_id = lax.broadcasted_iota(jnp.int32, (PAIR_ROWS, LANES), 0)
-    lane_id = lax.broadcasted_iota(jnp.int32, (PAIR_ROWS, LANES), 1)
-    for index, ref in enumerate(pair_refs):
-        hop = (index + 1) // 2
-        source = (chip + (-sign if index % 2 else sign) * hop + CHIPS) % CHIPS
-        start = pl.multiple_of(source * PAIR_ROWS, PAIR_ROWS)
+    core = where_ref[0] % 2
+    row_id = lax.broadcasted_iota(jnp.int32, (PIECE_ROWS, LANES), 0)
+    lane_id = lax.broadcasted_iota(jnp.int32, (PIECE_ROWS, LANES), 1)
+    for index, ref in enumerate(piece_refs):
+        distance, other = piece_of(index)
+        source = 2 * ((chip + distance + CHIPS) % CHIPS) + (1 - core if other else core)
+        start = pl.multiple_of(source * PIECE_ROWS, PIECE_ROWS)
         for block in range(BLOCKS):
-            values = ref[pl.ds(block, PAIR_ROWS, stride=BLOCKS), :]
+            values = ref[pl.ds(block, PIECE_ROWS, stride=BLOCKS), :]
             on_diagonal = row_id + start == lane_id + LANES * block
-            work[pl.ds(start, PAIR_ROWS), LANES * block:LANES * (block + 1)] = jnp.where(
+            work[pl.ds(start, PIECE_ROWS), LANES * block:LANES * (block + 1)] = jnp.where(
                 on_diagonal, values + damping, values
             )
     lane = lax.broadcasted_iota(jnp.int32, (8, LANES), 1)
@@ -160,24 +168,25 @@
             keep = row_id >= lane_id + LANES * block
             out_ref[pl.ds(block, ORDER, stride=BLOCKS), :] = jnp.where(keep, lower, 0.0)
 
-    @pl.when(jnp.logical_and(row > 0, col == 0))
+    @pl.when(jnp.logical_and(row >= col, row > 0))
     def _():
-        load(own_ref, row_high, row_low)
+        load(row_ref, row_high, row_low)
         for start, stop in GROUPS:
-            left = row_high[:, :stop], row_low[:, :stop]
-            result = product3(left, (high_ref[start:stop, :stop], low_ref[start:stop, :stop]), transposed=True)
-            for block in range(start // LANES, stop // LANES):
-                at = LANES * block - start
-                out_ref[pl.ds(block, ORDER, stride=BLOCKS), :] = result[:, at:at + LANES]
+            weights = high_ref[start:stop, :stop], low_ref[start:stop, :stop]
+            solved = product3(weights, (row_high[:stop, :], row_low[:stop, :])).T
+            left_high[:, start:stop], left_low[:, start:stop] = split(solved)
+
+            @pl.when(col == 0)
+            def _():
+                for block in range(start // LANES, stop // LANES):
+                    at = LANES * block - start
+                    out_ref[pl.ds(block, ORDER, stride=BLOCKS), :] = solved[:, at:at + LANES]
 
     @pl.when(jnp.logical_and(row >= col, col > 0))
     def _():
-        load(row_ref, row_high, row_low)
         load(col_ref, col_high, col_low)
         for start, stop in reversed(GROUPS):
             weights = high_ref[start:stop, :stop], low_ref[start:stop, :stop]
-            solved = product3(weights, (row_high[:stop, :], row_low[:stop, :]))
-            left_high[:, start:stop], left_low[:, start:stop] = split(solved.T)
             solved = product3(weights, (col_high[:stop, :], col_low[:stop, :]))
             col_high[start:stop, :], col_low[start:stop, :] = split(solved)
         added = jnp.where(row == col, damping_ref[0], 0.0)
@@ -198,7 +207,7 @@
 SMEM = pl.BlockSpec(memory_space=pltpu.SMEM)
 
 
-def factorize(where, damping, pairs):
+def factorize(where, damping, pieces):
     return pl.pallas_call(
         factor_kernel,
         out_shape=[
@@ -206,12 +215,12 @@
             jax.ShapeDtypeStruct((ORDER, ORDER), BF16),
             jax.ShapeDtypeStruct((ORDER, ORDER), F32),
         ],
-        in_specs=[SMEM, SMEM] + [VMEM] * CHIPS,
+        in_specs=[SMEM, SMEM] + [VMEM] * GRID,
         out_specs=[VMEM, VMEM, VMEM],
         scratch_shapes=[pltpu.VMEM((ORDER, ORDER), F32)],
         interpret=INTERPRET,
         name="factorize",
-    )(where, damping, *pairs)
+    )(where, damping, *pieces)
 
 
 def finish(where, damping, high, low, upper, row_tile, col_tile, own):
@@ -234,9 +243,11 @@
     size = own.shape[0] // chips
 
     piece = jnp.where(row == 0, own[:size], 0.0)
-    arrived = [
-        lax.ppermute(own[size * z:size * (z + 1)], "row", [(0, 2 * z)]) for z in SCATTER
-    ]
+    arrived = []
+    source = own
+    for z in SCATTER:
+        part, source = lax.optimization_barrier((source[size * z:size * (z + 1)], source))
+        arrived.append(lax.ppermute(part, "row", [(0, 2 * z)]))
     for other in arrived:
         piece = piece + other
 
@@ -246,36 +257,44 @@
     swap = [(r * GRID + c, c * GRID + r) for r in range(GRID) for c in range(GRID)]
     turned = lax.ppermute(half, ("row", "col"), swap)
 
-    moving = jnp.where(col == 0, piece, 0.0)
+    moving = jnp.where(col == 0, half, 0.0)
     for hop in (8, 4, 2, 1):
-        moving = moving + lax.ppermute(
-            moving, ("row", "col"),
-            [(2 * z * GRID + c, 2 * z * GRID + c + hop) for z in range(chips) for c in range(0, GRID, 2 * hop)],
-        )
-    moving = moving + lax.ppermute(moving, "row", [(2 * z, 2 * z + 1) for z in range(chips)])
-
-    other_core = [(r, r ^ 1) for r in range(GRID)]
-    onward = [(2 * z, 2 * ((z + 1) % chips)) for z in range(chips)]
-    onward += [(2 * z + 1, 2 * ((z - 1) % chips) + 1) for z in range(chips)]
-    pairs = [moving]
-    for hop in range(1, chips // 2 + 1):
-        moving = lax.ppermute(moving, "row", onward)
+        moving = moving + lax.ppermute(moving, "col", [(c, c + hop) for c in range(0, GRID, 2 * hop)])
+
+    def step(value, pairs):
+        return lax.ppermute(value, "row", pairs)
+
+    forth = [(r, (r + 2) % GRID) for r in range(GRID)]
+    back = [(r, (r - 2) % GRID) for r in range(GRID)]
+    across = [(r, r ^ 1) for r in range(GRID)]
+    ahead = behind = moving
+    pieces = [moving, step(moving, across)]
+    for hop in range(1, chips // 2):
+        ahead = step(ahead, forth)
+        behind = step(behind, back)
         if hop == 3:
-            moving, turned = lax.optimization_barrier((moving, turned))
-        pairs.append(moving)
-        if hop < chips // 2:
-            pairs.append(lax.ppermute(moving, "row", other_core))
+            behind, turned = lax.optimization_barrier((behind, turned))
+        pieces += [ahead, step(ahead, across), behind, step(behind, across)]
+    ahead = step(ahead, forth)
+    pieces += [ahead, step(ahead, across)]
     row_tile = lax.all_gather(turned, "col", axis=0, tiled=True)
-    return pairs, row_tile, col_tile
+    return pieces, row_tile, col_tile
+
+
+def piece_of(index):
+    if index < 2:
+        return 0, index
+    hop, kind = (index - 2) // 4 + 1, (index - 2) % 4
+    return (-hop, hop)[kind // 2], kind % 2
 
 
 def on_device(factor, damping):
     row = lax.axis_index("row")
     col = lax.axis_index("col")
     own = factor.reshape(FLAT, LANES)
-    pairs, row_tile, col_tile = spread(own)
+    pieces, row_tile, col_tile = spread(own)
     where = jnp.stack([row, col]).astype(jnp.int32)
-    high, low, upper = factorize(where, damping, pairs)
+    high, low, upper = factorize(where, damping, pieces)
     result = finish(where, damping, high, low, upper, row_tile, col_tile, own)
     return result.reshape(factor.shape)
 

time: 217 us -> 214 us (0.986)
  the two profiles are of different devices: /device:TPU:9 before, /device:TPU:139 now
where the time goes in v4:
time: 214 us
  waiting for transfers between devices  85.3 us (40%)
  Pallas kernels  66.1 us (31%)
  starting transfers between devices  40 us (19%)
  between operations  14.5 us (7%)
  local copies, waits for them, and re-layouts  4.3 us (2%)
  other arithmetic  3.65 us (2%)
    pallas_call x1, Pallas kernels, factorize(): pl.pallas_call(factor_kernel, out_shape=[jax.ShapeDtypeStruct((ORDER, ORD...  43.7 us
    ppermute x15, starting transfers between devices, step(): return lax.ppermute(value, 'row', pairs)  28.6 us
    ppermute x15, waiting for transfers between devices, step(): return lax.ppermute(value, 'row', pairs)  24.1 us
    ppermute x1, waiting for transfers between devices, spread(): lax.ppermute(piece[size // 2:], 'row', [(2 * z, 2 * z + 1) for z in range...  23.2 us
    pallas_call x1, Pallas kernels, finish(): pl.pallas_call(update_kernel, out_shape=jax.ShapeDtypeStruct((FLAT, LANES...  22.4 us
    ppermute x4, waiting for transfers between devices, spread(): lax.ppermute(moving, 'col', [(c, c + hop) for c in range(0, GRID, 2 * hop)])  20.5 us
    ppermute x1, waiting for transfers between devices, spread(): turned = lax.ppermute(half, ('row', 'col'), swap)  17.5 us
    ppermute x7, starting transfers between devices, spread(): arrived.append(lax.ppermute(part, 'row', [(0, 2 * z)]))  4.8 us
  transfers between devices with their start and end apart: 30, of which 7 were waited for; matrix products, arithmetic and copies ran while one was open for 0% of the time, Pallas kernels for 20%

profile of v4, /device:TPU:139, one launch (start us, length us, event | category | flops | bytes accessed | tf_op | source)
XLA Modules:
  0.0 213.8 jit_solution(13521013221609595746)
XLA Ops:
  6.5 2.0 broadcast_select_fusion
  8.5 1.0 slice.37
  9.5 1.0 slice.38
  10.7 0.7 collective-permute-start.6
  11.4 0.7 collective-permute-start.5
  12.1 0.7 collective-permute-start.4
  12.8 0.7 collective-permute-start.3
  13.5 0.7 collective-permute-start.2
  14.2 0.7 collective-permute-start.1
  14.9 0.7 collective-permute-start
  15.9 1.3 collective-permute-start.7
  17.2 23.2 %collective-permute-done.7 = f32[392,128]{1,0:T(8,128)S(1)} collective-permute-done((f32[392,128]{1,0:T(8,128)S(1)}, f32[392,128]{1,0:T(8,128)S(1)}, u32[]{:S(2)}, u32[]{:S(2)}) %collective-permute-start.7) | collective-permute-done | bytes 200736 | tf_op jit(solution)/shard_map/ppermute | solution.py:254
  40.4 0.7 broadcast_select_fusion.1
  41.2 0.7 collective-permute-start.8
  41.9 0.7 collective-permute-start.9
  42.6 0.7 collective-permute-start.10
  43.4 1.3 collective-permute-start.11
  44.7 20.5 %collective-permute-done.11 = f32[392,128]{1,0:T(8,128)S(1)} collective-permute-done((f32[392,128]{1,0:T(8,128)S(1)}, f32[392,128]{1,0:T(8,128)S(1)}, u32[]{:S(2)}, u32[]{:S(2)}) %collective-permute-start.11) | collective-permute-done | bytes 200736 | tf_op jit(solution)/shard_map/ppermute | solution.py:262
  65.3 6.8 %collective-permute-done.15.refs_4_ = f32[392,128]{1,0:T(8,128)S(1)} collective-permute-done((f32[392,128]{1,0:T(8,128)S(1)}, f32[392,128]{1,0:T(8,128)S(1)}, u32[]{:S(2)}, u32[]{:S(2)}) %collective-permute-start.15) | collective-permute-done | bytes 200736 | tf_op jit(solution)/shard_map/ppermute | solution.py:265
  72.1 2.8 %collective-permute-start.19 = (f32[392,128]{1,0:T(8,128)S(1)}, f32[392,128]{1,0:T(8,128)S(1)}, u32[]{:S(2)}, u32[]{:S(2)}) collective-permute-start(f32[392,128]{1,0:T(8,128)S(1)} %collective-permute-done.15.refs_4_), channel_id=1, source_target_pairs={{0,224},{16,240},{32,0},{48,16},{64,32},{80,48},{96,64},{112,80},{... | collective-permute-start | bytes 602120 | tf_op jit(solution)/shard_map/ppermute | solution.py:265
  74.9 1.9 collective-permute-start.24
  76.8 3.5 %collective-permute-done.19.refs_8_ = f32[392,128]{1,0:T(8,128)S(1)} collective-permute-done((f32[392,128]{1,0:T(8,128)S(1)}, f32[392,128]{1,0:T(8,128)S(1)}, u32[]{:S(2)}, u32[]{:S(2)}) %collective-permute-start.19) | collective-permute-done | bytes 200736 | tf_op jit(solution)/shard_map/ppermute | solution.py:265
  80.4 1.3 collective-permute-start.23
  81.7 17.5 %collective-permute-done.24 = f32[392,128]{1,0:T(8,128)S(1)} collective-permute-done((f32[392,128]{1,0:T(8,128)}, f32[392,128]{1,0:T(8,128)S(1)}, u32[]{:S(2)}, u32[]{:S(2)}) %collective-permute-start.24) | collective-permute-done | bytes 200736 | tf_op jit(solution)/shard_map/ppermute | solution.py:258
  99.2 0.7 copy-done.17
  100.0 5.8 %collective-permute-done.13.refs_2_ = f32[392,128]{1,0:T(8,128)S(1)} collective-permute-done((f32[392,128]{1,0:T(8,128)S(1)}, f32[392,128]{1,0:T(8,128)S(1)}, u32[]{:S(2)}, u32[]{:S(2)}) %collective-permute-start.13) | collective-permute-done | bytes 200736 | tf_op jit(solution)/shard_map/ppermute | solution.py:265
  105.8 7.9 %collective-permute-done.17.refs_6_ = f32[392,128]{1,0:T(8,128)S(1)} collective-permute-done((f32[392,128]{1,0:T(8,128)S(1)}, f32[392,128]{1,0:T(8,128)S(1)}, u32[]{:S(2)}, u32[]{:S(2)}) %collective-permute-start.17) | collective-permute-done | bytes 200736 | tf_op jit(solution)/shard_map/ppermute | solution.py:265
  113.7 8.6 %collective-permute-start.12 = (f32[392,128]{1,0:T(8,128)S(1)}, f32[392,128]{1,0:T(8,128)S(1)}, u32[]{:S(2)}, u32[]{:S(2)}) collective-permute-start(f32[392,128]{1,0:T(8,128)S(1)} %add.48.refs_0_), channel_id=1, source_target_pairs={{0,16},{16,0},{32,48},{48,32},{64,80},{80,64},{96,112},{112,96},{1... | collective-permute-start | bytes 602120 | tf_op jit(solution)/shard_map/ppermute | solution.py:265
  122.9 8.2 %collective-permute-start.18 = (f32[392,128]{1,0:T(8,128)S(1)}, f32[392,128]{1,0:T(8,128)S(1)}, u32[]{:S(2)}, u32[]{:S(2)}) collective-permute-start(f32[392,128]{1,0:T(8,128)S(1)} %collective-permute-done.17.refs_6_), channel_id=1, source_target_pairs={{0,16},{16,0},{32,48},{48,32},{64,80},{80,64},{96,112},{112,96},{1... | collective-permute-start | bytes 602120 | tf_op jit(solution)/shard_map/ppermute | solution.py:265
  131.7 6.3 %collective-permute-start.27 = (f32[392,128]{1,0:T(8,128)S(1)}, f32[392,128]{1,0:T(8,128)S(1)}, u32[]{:S(2)}, u32[]{:S(2)}) collective-permute-start(f32[392,128]{1,0:T(8,128)S(1)} %collective-permute-done.26.refs_14_), channel_id=1, source_target_pairs={{0,16},{16,0},{32,48},{48,32},{64,80},{80,64},{96,112},{112,96},{1... | collective-permute-start | bytes 602120 | tf_op jit(solution)/shard_map/ppermute | solution.py:265
  140.9 43.7 %factorize.1 = (bf16[896,896]{1,0:T(8,128)(2,1)}, bf16[896,896]{1,0:T(8,128)(2,1)}, f32[896,896]{1,0:T(8,128)}) custom-call(s32[2]{0:T(128)} %pad_add_fusion.where_ref, f32[1]{0:T(128)S(6)} %copy.4.damping_ref, f32[392,128]{1,0:T(8,128)} %copy-done.1, f32[392,128]{1,0:T(8,128)} %copy-done.8, f32[392,128]{1,0:T(8,128)} %copy-done.5, f32[392,128]{1,0:T(8,128)} %copy-done.9, ...), custom_call_target="tpu_custom_call" | custom-call | tf_op jit(solution)/shard_map/factorize/pallas_call | solution.py:211
  184.6 22.4 %finish.1 = f32[6272,128]{1,0:T(8,128)} custom-call(s32[2]{0:T(128)} %pad_add_fusion.where_ref, f32[1]{0:T(128)S(6)} %copy.4.damping_ref, bf16[896,896]{1,0:T(8,128)(2,1)} %get-tuple-element.37.high_ref, bf16[896,896]{1,0:T(8,128)(2,1)} %get-tuple-element.38.low_ref, f32[896,896]{1,0:T(8,128)} %get-tuple-element.39.upper_ref, ...), custom_call_target="tpu_custom_call" | custom-call | tf_op jit(solution)/shard_map/finish/pallas_call | solution.py:227
  (83 shorter events, 4.0 us)
Async XLA Ops:
  6.5 178.1 %all-gather.5.cloned.1.call-start = ((), (), s32[]{:S(2)}) async-start(), calls=%async_computation.1 | async-start | bytes 3411968 | tf_op jit(solution)/shard_map/all_gather | solution.py:256
  10.7 3.5 %collective-permute-start.6 = (f32[784,128]{1,0:T(8,128)S(1)}, f32[784,128]{1,0:T(8,128)S(1)}, u32[]{:S(2)}, u32[]{:S(2)}) collective-permute-start(f32[784,128]{1,0:T(8,128)S(1)} %slice.42), channel_id=1, source_target_pairs={{0,224},{1,225},{2,226},{3,227},{4,228},{5,229},{6,230},{7,231},{8... | collective-permute-start | bytes 1204232 | tf_op jit(solution)/shard_map/ppermute | solution.py:250
  11.4 3.5 %collective-permute-start.5 = (f32[784,128]{1,0:T(8,128)S(1)}, f32[784,128]{1,0:T(8,128)S(1)}, u32[]{:S(2)}, u32[]{:S(2)}) collective-permute-start(f32[784,128]{1,0:T(8,128)S(1)} %slice.41), channel_id=1, source_target_pairs={{0,32},{1,33},{2,34},{3,35},{4,36},{5,37},{6,38},{7,39},{8,40},{9,... | collective-permute-start | bytes 1204232 | tf_op jit(solution)/shard_map/ppermute | solution.py:250
  12.1 3.5 %collective-permute-start.4 = (f32[784,128]{1,0:T(8,128)S(1)}, f32[784,128]{1,0:T(8,128)S(1)}, u32[]{:S(2)}, u32[]{:S(2)}) collective-permute-start(f32[784,128]{1,0:T(8,128)S(1)} %slice.40), channel_id=1, source_target_pairs={{0,192},{1,193},{2,194},{3,195},{4,196},{5,197},{6,198},{7,199},{8... | collective-permute-start | bytes 1204232 | tf_op jit(solution)/shard_map/ppermute | solution.py:250
  12.8 2.8 %collective-permute-start.3 = (f32[784,128]{1,0:T(8,128)S(1)}, f32[784,128]{1,0:T(8,128)S(1)}, u32[]{:S(2)}, u32[]{:S(2)}) collective-permute-start(f32[784,128]{1,0:T(8,128)S(1)} %slice.39), channel_id=1, source_target_pairs={{0,64},{1,65},{2,66},{3,67},{4,68},{5,69},{6,70},{7,71},{8,72},{9,... | collective-permute-start | bytes 1204232 | tf_op jit(solution)/shard_map/ppermute | solution.py:250
  13.5 2.1 collective-permute-start.2
  14.2 1.4 collective-permute-start.1
  14.9 0.7 collective-permute-start
  15.9 24.5 %collective-permute-start.7 = (f32[392,128]{1,0:T(8,128)S(1)}, f32[392,128]{1,0:T(8,128)S(1)}, u32[]{:S(2)}, u32[]{:S(2)}) collective-permute-start(f32[392,128]{1,0:T(8,128)S(1)} %slice.46), channel_id=1, source_target_pairs={{0,16},{32,48},{64,80},{96,112},{128,144},{160,176},{192,208},{224... | collective-permute-start | bytes 602120 | tf_op jit(solution)/shard_map/ppermute | solution.py:254
  41.1 143.5 %all-gather.3.cloned.1.call-start = ((), (), s32[]{:S(2)}) async-start(), calls=%async_computation | async-start | bytes 3411968 | tf_op jit(solution)/shard_map/all_gather | solution.py:280
  41.2 0.7 collective-permute-start.8
  41.9 0.7 collective-permute-start.9
  42.6 0.7 collective-permute-start.10
  43.4 21.8 %collective-permute-start.11 = (f32[392,128]{1,0:T(8,128)S(1)}, f32[392,128]{1,0:T(8,128)S(1)}, u32[]{:S(2)}, u32[]{:S(2)}) collective-permute-start(f32[392,128]{1,0:T(8,128)S(1)} %add.47), channel_id=1, source_target_pairs={{0,1},{2,3},{4,5},{6,7},{8,9},{10,11},{12,13},{14,15},{16,17},{18,... | collective-permute-start | bytes 602120 | tf_op jit(solution)/shard_map/ppermute | solution.py:262
  65.2 74.2 %copy-start.1 = (f32[392,128]{1,0:T(8,128)}, f32[392,128]{1,0:T(8,128)S(1)}, u32[]{:S(2)}) copy-start(f32[392,128]{1,0:T(8,128)S(1)} %add.48.refs_0_) | copy-start | bytes 602116
  65.2 6.9 %collective-permute-start.15 = (f32[392,128]{1,0:T(8,128)S(1)}, f32[392,128]{1,0:T(8,128)S(1)}, u32[]{:S(2)}, u32[]{:S(2)}) collective-permute-start(f32[392,128]{1,0:T(8,128)S(1)} %add.48.refs_0_), channel_id=1, source_target_pairs={{0,224},{16,240},{32,0},{48,16},{64,32},{80,48},{96,64},{112,80},{... | collective-permute-start | bytes 602120 | tf_op jit(solution)/shard_map/ppermute | solution.py:265
  72.1 67.3 %copy-start.2 = (f32[392,128]{1,0:T(8,128)}, f32[392,128]{1,0:T(8,128)S(1)}, u32[]{:S(2)}) copy-start(f32[392,128]{1,0:T(8,128)S(1)} %collective-permute-done.15.refs_4_) | copy-start | bytes 602116
  72.1 8.3 %collective-permute-start.19 = (f32[392,128]{1,0:T(8,128)S(1)}, f32[392,128]{1,0:T(8,128)S(1)}, u32[]{:S(2)}, u32[]{:S(2)}) collective-permute-start(f32[392,128]{1,0:T(8,128)S(1)} %collective-permute-done.15.refs_4_), channel_id=1, source_target_pairs={{0,224},{16,240},{32,0},{48,16},{64,32},{80,48},{96,64},{112,80},{... | collective-permute-start | bytes 602120 | tf_op jit(solution)/shard_map/ppermute | solution.py:265
  74.9 24.3 %collective-permute-start.24 = (f32[392,128]{1,0:T(8,128)}, f32[392,128]{1,0:T(8,128)S(1)}, u32[]{:S(2)}, u32[]{:S(2)}) collective-permute-start(f32[392,128]{1,0:T(8,128)} %get-tuple-element.42), channel_id=1, source_target_pairs={{0,0},{1,16},{2,32},{3,48},{4,64},{5,80},{6,96},{7,112},{8,128},{9... | collective-permute-start | bytes 602120 | tf_op jit(solution)/shard_map/ppermute | solution.py:258
  80.4 18.8 %collective-permute-start.23 = (f32[392,128]{1,0:T(8,128)S(1)}, f32[392,128]{1,0:T(8,128)S(1)}, u32[]{:S(2)}, u32[]{:S(2)}) collective-permute-start(f32[392,128]{1,0:T(8,128)S(1)} %collective-permute-done.19.refs_8_), channel_id=1, source_target_pairs={{0,224},{16,240},{32,0},{48,16},{64,32},{80,48},{96,64},{112,80},{... | collective-permute-start | bytes 602120 | tf_op jit(solution)/shard_map/ppermute | solution.py:265
  99.9 5.9 %collective-permute-start.13 = (f32[392,128]{1,0:T(8,128)S(1)}, f32[392,128]{1,0:T(8,128)S(1)}, u32[]{:S(2)}, u32[]{:S(2)}) collective-permute-start(f32[392,128]{1,0:T(8,128)S(1)} %add.48.refs_0_), channel_id=1, source_target_pairs={{0,32},{16,48},{32,64},{48,80},{64,96},{80,112},{96,128},{112,144}... | collective-permute-start | bytes 602120 | tf_op jit(solution)/shard_map/ppermute | solution.py:265
  105.8 7.9 %collective-permute-start.17 = (f32[392,128]{1,0:T(8,128)S(1)}, f32[392,128]{1,0:T(8,128)S(1)}, u32[]{:S(2)}, u32[]{:S(2)}) collective-permute-start(f32[392,128]{1,0:T(8,128)S(1)} %collective-permute-done.13.refs_2_), channel_id=1, source_target_pairs={{0,32},{16,48},{32,64},{48,80},{64,96},{80,112},{96,128},{112,144}... | collective-permute-start | bytes 602120 | tf_op jit(solution)/shard_map/ppermute | solution.py:265
  113.7 9.1 %collective-permute-start.21 = (f32[392,128]{1,0:T(8,128)S(1)}, f32[392,128]{1,0:T(8,128)S(1)}, u32[]{:S(2)}, u32[]{:S(2)}) collective-permute-start(f32[392,128]{1,0:T(8,128)S(1)} %collective-permute-done.17.refs_6_), channel_id=1, source_target_pairs={{0,32},{16,48},{32,64},{48,80},{64,96},{80,112},{96,128},{112,144}... | collective-permute-start | bytes 602120 | tf_op jit(solution)/shard_map/ppermute | solution.py:265
  113.7 17.4 %collective-permute-start.12 = (f32[392,128]{1,0:T(8,128)S(1)}, f32[392,128]{1,0:T(8,128)S(1)}, u32[]{:S(2)}, u32[]{:S(2)}) collective-permute-start(f32[392,128]{1,0:T(8,128)S(1)} %add.48.refs_0_), channel_id=1, source_target_pairs={{0,16},{16,0},{32,48},{48,32},{64,80},{80,64},{96,112},{112,96},{1... | collective-permute-start | bytes 602120 | tf_op jit(solution)/shard_map/ppermute | solution.py:265
  122.3 8.8 %collective-permute-start.14 = (f32[392,128]{1,0:T(8,128)S(1)}, f32[392,128]{1,0:T(8,128)S(1)}, u32[]{:S(2)}, u32[]{:S(2)}) collective-permute-start(f32[392,128]{1,0:T(8,128)S(1)} %collective-permute-done.13.refs_2_), channel_id=1, source_target_pairs={{0,16},{16,0},{32,48},{48,32},{64,80},{80,64},{96,112},{112,96},{1... | collective-permute-start | bytes 602120 | tf_op jit(solution)/shard_map/ppermute | solution.py:265
  122.4 9.2 %collective-permute-start.16 = (f32[392,128]{1,0:T(8,128)S(1)}, f32[392,128]{1,0:T(8,128)S(1)}, u32[]{:S(2)}, u32[]{:S(2)}) collective-permute-start(f32[392,128]{1,0:T(8,128)S(1)} %collective-permute-done.15.refs_4_), channel_id=1, source_target_pairs={{0,16},{16,0},{32,48},{48,32},{64,80},{80,64},{96,112},{112,96},{1... | collective-permute-start | bytes 602120 | tf_op jit(solution)/shard_map/ppermute | solution.py:265
  122.9 8.9 %collective-permute-start.26 = (f32[392,128]{1,0:T(8,128)S(1)}, f32[392,128]{1,0:T(8,128)S(1)}, u32[]{:S(2)}, u32[]{:S(2)}) collective-permute-start(f32[392,128]{1,0:T(8,128)S(1)} %collective-permute-done.21.refs_10_), channel_id=1, source_target_pairs={{0,32},{16,48},{32,64},{48,80},{64,96},{80,112},{96,128},{112,144}... | collective-permute-start | bytes 602120 | tf_op jit(solution)/shard_map/ppermute | solution.py:265
  122.9 16.4 %collective-permute-start.18 = (f32[392,128]{1,0:T(8,128)S(1)}, f32[392,128]{1,0:T(8,128)S(1)}, u32[]{:S(2)}, u32[]{:S(2)}) collective-permute-start(f32[392,128]{1,0:T(8,128)S(1)} %collective-permute-done.17.refs_6_), channel_id=1, source_target_pairs={{0,16},{16,0},{32,48},{48,32},{64,80},{80,64},{96,112},{112,96},{1... | collective-permute-start | bytes 602120 | tf_op jit(solution)/shard_map/ppermute | solution.py:265
  131.1 8.2 %collective-permute-start.20 = (f32[392,128]{1,0:T(8,128)S(1)}, f32[392,128]{1,0:T(8,128)S(1)}, u32[]{:S(2)}, u32[]{:S(2)}) collective-permute-start(f32[392,128]{1,0:T(8,128)S(1)} %collective-permute-done.19.refs_8_), channel_id=1, source_target_pairs={{0,16},{16,0},{32,48},{48,32},{64,80},{80,64},{96,112},{112,96},{1... | collective-permute-start | bytes 602120 | tf_op jit(solution)/shard_map/ppermute | solution.py:265
  131.2 8.1 %collective-permute-start.25 = (f32[392,128]{1,0:T(8,128)S(1)}, f32[392,128]{1,0:T(8,128)S(1)}, u32[]{:S(2)}, u32[]{:S(2)}) collective-permute-start(f32[392,128]{1,0:T(8,128)S(1)} %collective-permute-done.23.refs_12_), channel_id=1, source_target_pairs={{0,16},{16,0},{32,48},{48,32},{64,80},{80,64},{96,112},{112,96},{1... | collective-permute-start | bytes 602120 | tf_op jit(solution)/shard_map/ppermute | solution.py:265
  131.6 7.7 %collective-permute-start.22 = (f32[392,128]{1,0:T(8,128)S(1)}, f32[392,128]{1,0:T(8,128)S(1)}, u32[]{:S(2)}, u32[]{:S(2)}) collective-permute-start(f32[392,128]{1,0:T(8,128)S(1)} %collective-permute-done.21.refs_10_), channel_id=1, source_target_pairs={{0,16},{16,0},{32,48},{48,32},{64,80},{80,64},{96,112},{112,96},{1... | collective-permute-start | bytes 602120 | tf_op jit(solution)/shard_map/ppermute | solution.py:265
  131.7 7.7 %collective-permute-start.27 = (f32[392,128]{1,0:T(8,128)S(1)}, f32[392,128]{1,0:T(8,128)S(1)}, u32[]{:S(2)}, u32[]{:S(2)}) collective-permute-start(f32[392,128]{1,0:T(8,128)S(1)} %collective-permute-done.26.refs_14_), channel_id=1, source_target_pairs={{0,16},{16,0},{32,48},{48,32},{64,80},{80,64},{96,112},{112,96},{1... | collective-permute-start | bytes 602120 | tf_op jit(solution)/shard_map/ppermute | solution.py:265
  (16 other events, 215.9 us)
Sparse Core Ops, SparseCore 0:
  41.3 40.7 all-gather.4
  100.0 58.2 all-gather.2

commit v5 on v4

--- a/solution.py
+++ b/solution.py
@@ -91,8 +91,21 @@
     return mixed, corner
 
 
+def load_turned(ref, high, low):
+    for block in range(BLOCKS):
+        down = slice(LANES * block, LANES * (block + 1))
+        high[down, :], low[down, :] = split(ref[pl.ds(block, ORDER, stride=BLOCKS), :].T)
+
+
+def solve(tile, inverse, start, stop):
+    (high, low), (inverse_high, inverse_low) = tile, inverse
+    weights = inverse_high[start:stop, :stop], inverse_low[start:stop, :stop]
+    return product3((high[:, :stop], low[:, :stop]), weights, transposed=True)
+
+
 def factor_kernel(where_ref, damping_ref, *refs):
-    piece_refs, (high_ref, low_ref, upper_ref, work) = refs[:GRID], refs[GRID:]
+    piece_refs, col_ref, (high_ref, low_ref, upper_ref, right_high, right_low) = refs[:GRID], refs[GRID], refs[GRID + 1:GRID + 6]
+    work, left_high, left_low, panel, tile_high, tile_low = refs[GRID + 6:]
     damping = damping_ref[0]
     chip = where_ref[0] // 2
     core = where_ref[0] % 2
@@ -117,18 +130,27 @@
         mixed, corner = factor_block(slabs)
         inverse = jnp.concatenate([jnp.where(lane < 8 * i + 8, mixed[i], 0.0) for i in range(16)], axis=0)
         upper = jnp.concatenate([jnp.where(lane < 8 * i + 8, corner[i], mixed[i]) for i in range(16)], axis=0)
-        inverse_parts = split(inverse)
-        work[here, :] = product3(inverse_parts, split(work[here, :]))
+        high, low = split(inverse)
+        stacked = jnp.concatenate([high, low], axis=1)
+        column_high, column_low = split(work[:, here])
+        column = product(jnp.concatenate([column_high, column_high], axis=1), stacked, True)
+        column = column + product(column_low, high, True)
+        left_high[...], left_low[...] = split(column)
+        work[here, :] = product3((high, low), split(work[here, :]))
         upper_ref[here, :] = work[here, :]
         upper_ref[here, here] = upper
         work[here, here] = inverse
-        panel_parts = split(work[here, :])
+        high, low = split(work[here, :])
+        panel[:LANES, :] = high
+        panel[LANES:, :] = low
 
         def update(i, inner):
             there = pl.ds(pl.multiple_of(i * LANES, LANES), LANES)
-            column = product3(split(work[there, here]), inverse_parts, transposed=True)
+            left = left_high[there, :]
+            change = product(jnp.concatenate([left, left], axis=1), panel[...], False)
+            change = change + product(left_low[there, :], panel[:LANES, :], False)
             work[there, here] = jnp.zeros((LANES, LANES), F32)
-            work[there, :] = work[there, :] - product3(split(column), panel_parts)
+            work[there, :] = work[there, :] - change
             return inner
 
         lax.fori_loop(k + 1, BLOCKS, update, 0)
@@ -143,17 +165,19 @@
         high_ref[down, :] = high
         low_ref[down, :] = low
 
+    @pl.when(jnp.logical_and(where_ref[0] >= where_ref[1], where_ref[1] > 0))
+    def _():
+        load_turned(col_ref, tile_high, tile_low)
+        for start, stop in GROUPS:
+            solved = solve((tile_high, tile_low), (high_ref, low_ref), start, stop).T
+            right_high[start:stop, :], right_low[start:stop, :] = split(solved)
+
 
 def update_kernel(
-    where_ref, damping_ref, high_ref, low_ref, upper_ref, row_ref, col_ref, own_ref, out_ref,
-    row_high, row_low, col_high, col_low, left_high, left_low,
+    where_ref, damping_ref, high_ref, low_ref, upper_ref, right_high, right_low, row_ref, own_ref, out_ref,
+    tile_high, tile_low, left_high, left_low,
 ):
     row, col = where_ref[0], where_ref[1]
-
-    def load(ref, high, low):
-        for block in range(BLOCKS):
-            lanes = slice(LANES * block, LANES * (block + 1))
-            high[:, lanes], low[:, lanes] = split(ref[pl.ds(block, ORDER, stride=BLOCKS), :])
 
     @pl.when(row < col)
     def _():
@@ -170,31 +194,23 @@
 
     @pl.when(jnp.logical_and(row >= col, row > 0))
     def _():
-        load(row_ref, row_high, row_low)
+        load_turned(row_ref, tile_high, tile_low)
         for start, stop in GROUPS:
-            weights = high_ref[start:stop, :stop], low_ref[start:stop, :stop]
-            solved = product3(weights, (row_high[:stop, :], row_low[:stop, :])).T
+            solved = solve((tile_high, tile_low), (high_ref, low_ref), start, stop)
             left_high[:, start:stop], left_low[:, start:stop] = split(solved)
 
-            @pl.when(col == 0)
-            def _():
-                for block in range(start // LANES, stop // LANES):
-                    at = LANES * block - start
-                    out_ref[pl.ds(block, ORDER, stride=BLOCKS), :] = solved[:, at:at + LANES]
+            for block in range(start // LANES, stop // LANES):
+                at = LANES * block - start
+                out_ref[pl.ds(block, ORDER, stride=BLOCKS), :] = solved[:, at:at + LANES]
 
     @pl.when(jnp.logical_and(row >= col, col > 0))
     def _():
-        load(col_ref, col_high, col_low)
-        for start, stop in reversed(GROUPS):
-            weights = high_ref[start:stop, :stop], low_ref[start:stop, :stop]
-            solved = product3(weights, (col_high[:stop, :], col_low[:stop, :]))
-            col_high[start:stop, :], col_low[start:stop, :] = split(solved)
         added = jnp.where(row == col, damping_ref[0], 0.0)
         row_id = lax.broadcasted_iota(jnp.int32, (ORDER, LANES), 0)
         lane_id = lax.broadcasted_iota(jnp.int32, (ORDER, LANES), 1)
         for start, stop in GROUPS:
             left = left_high[...], left_low[...]
-            result = product3(left, (col_high[:, start:stop], col_low[:, start:stop]))
+            result = product3(left, (right_high[:, start:stop], right_low[:, start:stop]))
             for block in range(start // LANES, stop // LANES):
                 at = LANES * block - start
                 place = pl.ds(block, ORDER, stride=BLOCKS)
@@ -207,32 +223,41 @@
 SMEM = pl.BlockSpec(memory_space=pltpu.SMEM)
 
 
-def factorize(where, damping, pieces):
+def factorize(where, damping, pieces, col_tile):
     return pl.pallas_call(
         factor_kernel,
         out_shape=[
             jax.ShapeDtypeStruct((ORDER, ORDER), BF16),
             jax.ShapeDtypeStruct((ORDER, ORDER), BF16),
             jax.ShapeDtypeStruct((ORDER, ORDER), F32),
+            jax.ShapeDtypeStruct((ORDER, ORDER), BF16),
+            jax.ShapeDtypeStruct((ORDER, ORDER), BF16),
         ],
-        in_specs=[SMEM, SMEM] + [VMEM] * GRID,
-        out_specs=[VMEM, VMEM, VMEM],
-        scratch_shapes=[pltpu.VMEM((ORDER, ORDER), F32)],
+        in_specs=[SMEM, SMEM] + [VMEM] * (GRID + 1),
+        out_specs=[VMEM] * 5,
+        scratch_shapes=[
+            pltpu.VMEM((ORDER, ORDER), F32),
+            pltpu.VMEM((ORDER, LANES), BF16),
+            pltpu.VMEM((ORDER, LANES), BF16),
+            pltpu.VMEM((2 * LANES, ORDER), BF16),
+            pltpu.VMEM((ORDER, ORDER), BF16),
+            pltpu.VMEM((ORDER, ORDER), BF16),
+        ],
         interpret=INTERPRET,
         name="factorize",
-    )(where, damping, *pieces)
-
-
-def finish(where, damping, high, low, upper, row_tile, col_tile, own):
+    )(where, damping, *pieces, col_tile)
+
+
+def finish(where, damping, factors, row_tile, own):
     return pl.pallas_call(
         update_kernel,
         out_shape=jax.ShapeDtypeStruct((FLAT, LANES), F32),
-        in_specs=[SMEM, SMEM] + [VMEM] * 6,
+        in_specs=[SMEM, SMEM] + [VMEM] * 7,
         out_specs=VMEM,
-        scratch_shapes=[pltpu.VMEM((ORDER, ORDER), BF16)] * 6,
+        scratch_shapes=[pltpu.VMEM((ORDER, ORDER), BF16)] * 4,
         interpret=INTERPRET,
         name="finish",
-    )(where, damping, high, low, upper, row_tile, col_tile, own)
+    )(where, damping, *factors, row_tile, own)
 
 
 def spread(own):
@@ -294,8 +319,8 @@
     own = factor.reshape(FLAT, LANES)
     pieces, row_tile, col_tile = spread(own)
     where = jnp.stack([row, col]).astype(jnp.int32)
-    high, low, upper = factorize(where, damping, pieces)
-    result = finish(where, damping, high, low, upper, row_tile, col_tile, own)
+    factors = factorize(where, damping, pieces, col_tile)
+    result = finish(where, damping, factors, row_tile, own)
     return result.reshape(factor.shape)
 
 

time: 214 us -> 209 us (0.977)
  Pallas kernels: 66.1 us -> 61.4 us
    pallas_call x1, Pallas kernels: 22.4 us -> 16.9 us  [finish(): pl.pallas_call(update_kernel, out_shape=jax.ShapeDtypeStruct((FLAT, LANES...]
  transfers between devices with their start and end apart: 30 -> 30, of which waited for: 7 -> 7; matrix products, arithmetic and copies ran while one was open for 0% -> 0% of each run, Pallas kernels for 20% -> 21%
where the time goes in v5:
time: 209 us; the launch traced here: 208 us
  waiting for transfers between devices  85.3 us (41%)
  Pallas kernels  61.4 us (29%)
  starting transfers between devices  40 us (19%)
  between operations  14.5 us (7%)
  local copies, waits for them, and re-layouts  3.68 us (2%)
  other arithmetic  3.6 us (2%)
    pallas_call x1, Pallas kernels, factorize(): pl.pallas_call(factor_kernel, out_shape=[jax.ShapeDtypeStruct((ORDER, ORD...  44.5 us
    ppermute x15, starting transfers between devices, step(): return lax.ppermute(value, 'row', pairs)  28.6 us
    ppermute x15, waiting for transfers between devices, step(): return lax.ppermute(value, 'row', pairs)  24.1 us
    ppermute x1, waiting for transfers between devices, spread(): lax.ppermute(piece[size // 2:], 'row', [(2 * z, 2 * z + 1) for z in range...  23.2 us
    ppermute x4, waiting for transfers between devices, spread(): lax.ppermute(moving, 'col', [(c, c + hop) for c in range(0, GRID, 2 * hop)])  20.5 us
    ppermute x1, waiting for transfers between devices, spread(): turned = lax.ppermute(half, ('row', 'col'), swap)  17.5 us
    pallas_call x1, Pallas kernels, finish(): pl.pallas_call(update_kernel, out_shape=jax.ShapeDtypeStruct((FLAT, LANES...  16.9 us
    ppermute x7, starting transfers between devices, spread(): arrived.append(lax.ppermute(part, 'row', [(0, 2 * z)]))  4.8 us
  transfers between devices with their start and end apart: 30, of which 7 were waited for; matrix products, arithmetic and copies ran while one was open for 0% of the time, Pallas kernels for 21%

profile of v5, /device:TPU:139, one launch (start us, length us, event | category | flops | bytes accessed | tf_op | source)
XLA Modules:
  0.0 208.5 jit_solution(3118994510866391449)
XLA Ops:
  6.5 2.0 broadcast_select_fusion
  8.5 1.0 slice.37
  9.5 1.0 slice.38
  10.7 0.7 collective-permute-start.6
  11.4 0.7 collective-permute-start.5
  12.1 0.7 collective-permute-start.4
  12.8 0.7 collective-permute-start.3
  13.5 0.7 collective-permute-start.2
  14.2 0.7 collective-permute-start.1
  14.9 0.7 collective-permute-start
  15.9 1.3 collective-permute-start.7
  17.2 23.2 %collective-permute-done.7 = f32[392,128]{1,0:T(8,128)S(1)} collective-permute-done((f32[392,128]{1,0:T(8,128)S(1)}, f32[392,128]{1,0:T(8,128)S(1)}, u32[]{:S(2)}, u32[]{:S(2)}) %collective-permute-start.7) | collective-permute-done | bytes 200736 | tf_op jit(solution)/shard_map/ppermute | solution.py:279
  40.4 0.7 broadcast_select_fusion.1
  41.2 0.7 collective-permute-start.8
  41.9 0.7 collective-permute-start.9
  42.6 0.7 collective-permute-start.10
  43.4 1.3 collective-permute-start.11
  44.7 20.5 %collective-permute-done.11 = f32[392,128]{1,0:T(8,128)S(1)} collective-permute-done((f32[392,128]{1,0:T(8,128)S(1)}, f32[392,128]{1,0:T(8,128)S(1)}, u32[]{:S(2)}, u32[]{:S(2)}) %collective-permute-start.11) | collective-permute-done | bytes 200736 | tf_op jit(solution)/shard_map/ppermute | solution.py:287
  65.3 6.8 %collective-permute-done.15.refs_4_ = f32[392,128]{1,0:T(8,128)S(1)} collective-permute-done((f32[392,128]{1,0:T(8,128)S(1)}, f32[392,128]{1,0:T(8,128)S(1)}, u32[]{:S(2)}, u32[]{:S(2)}) %collective-permute-start.15) | collective-permute-done | bytes 200736 | tf_op jit(solution)/shard_map/ppermute | solution.py:290
  72.1 2.8 %collective-permute-start.19 = (f32[392,128]{1,0:T(8,128)S(1)}, f32[392,128]{1,0:T(8,128)S(1)}, u32[]{:S(2)}, u32[]{:S(2)}) collective-permute-start(f32[392,128]{1,0:T(8,128)S(1)} %collective-permute-done.15.refs_4_), channel_id=1, source_target_pairs={{0,224},{16,240},{32,0},{48,16},{64,32},{80,48},{96,64},{112,80},{... | collective-permute-start | bytes 602120 | tf_op jit(solution)/shard_map/ppermute | solution.py:290
  74.9 1.9 collective-permute-start.24
  76.8 3.5 %collective-permute-done.19.refs_8_ = f32[392,128]{1,0:T(8,128)S(1)} collective-permute-done((f32[392,128]{1,0:T(8,128)S(1)}, f32[392,128]{1,0:T(8,128)S(1)}, u32[]{:S(2)}, u32[]{:S(2)}) %collective-permute-start.19) | collective-permute-done | bytes 200736 | tf_op jit(solution)/shard_map/ppermute | solution.py:290
  80.4 1.3 collective-permute-start.23
  81.7 17.5 %collective-permute-done.24 = f32[392,128]{1,0:T(8,128)S(1)} collective-permute-done((f32[392,128]{1,0:T(8,128)}, f32[392,128]{1,0:T(8,128)S(1)}, u32[]{:S(2)}, u32[]{:S(2)}) %collective-permute-start.24) | collective-permute-done | bytes 200736 | tf_op jit(solution)/shard_map/ppermute | solution.py:283
  99.2 0.7 copy-done.2
  100.0 5.8 %collective-permute-done.13.refs_2_ = f32[392,128]{1,0:T(8,128)S(1)} collective-permute-done((f32[392,128]{1,0:T(8,128)S(1)}, f32[392,128]{1,0:T(8,128)S(1)}, u32[]{:S(2)}, u32[]{:S(2)}) %collective-permute-start.13) | collective-permute-done | bytes 200736 | tf_op jit(solution)/shard_map/ppermute | solution.py:290
  105.8 7.9 %collective-permute-done.17.refs_6_ = f32[392,128]{1,0:T(8,128)S(1)} collective-permute-done((f32[392,128]{1,0:T(8,128)S(1)}, f32[392,128]{1,0:T(8,128)S(1)}, u32[]{:S(2)}, u32[]{:S(2)}) %collective-permute-start.17) | collective-permute-done | bytes 200736 | tf_op jit(solution)/shard_map/ppermute | solution.py:290
  113.7 8.6 %collective-permute-start.12 = (f32[392,128]{1,0:T(8,128)S(1)}, f32[392,128]{1,0:T(8,128)S(1)}, u32[]{:S(2)}, u32[]{:S(2)}) collective-permute-start(f32[392,128]{1,0:T(8,128)S(1)} %add.48.refs_0_), channel_id=1, source_target_pairs={{0,16},{16,0},{32,48},{48,32},{64,80},{80,64},{96,112},{112,96},{1... | collective-permute-start | bytes 602120 | tf_op jit(solution)/shard_map/ppermute | solution.py:290
  122.9 8.2 %collective-permute-start.18 = (f32[392,128]{1,0:T(8,128)S(1)}, f32[392,128]{1,0:T(8,128)S(1)}, u32[]{:S(2)}, u32[]{:S(2)}) collective-permute-start(f32[392,128]{1,0:T(8,128)S(1)} %collective-permute-done.17.refs_6_), channel_id=1, source_target_pairs={{0,16},{16,0},{32,48},{48,32},{64,80},{80,64},{96,112},{112,96},{1... | collective-permute-start | bytes 602120 | tf_op jit(solution)/shard_map/ppermute | solution.py:290
  131.7 6.3 %collective-permute-start.27 = (f32[392,128]{1,0:T(8,128)S(1)}, f32[392,128]{1,0:T(8,128)S(1)}, u32[]{:S(2)}, u32[]{:S(2)}) collective-permute-start(f32[392,128]{1,0:T(8,128)S(1)} %collective-permute-done.26.refs_14_), channel_id=1, source_target_pairs={{0,16},{16,0},{32,48},{48,32},{64,80},{80,64},{96,112},{112,96},{1... | collective-permute-start | bytes 602120 | tf_op jit(solution)/shard_map/ppermute | solution.py:290
  140.2 44.5 %factorize.1 = (bf16[896,896]{1,0:T(8,128)(2,1)}, bf16[896,896]{1,0:T(8,128)(2,1)}, f32[896,896]{1,0:T(8,128)}, bf16[896,896]{1,0:T(8,128)(2,1)}, bf16[896,896]{1,0:T(8,128)(2,1)}) custom-call(s32[2]{0:T(128)} %pad_add_fusion.where_ref, f32[1]{0:T(128)S(6)} %copy.4.damping_ref, f32[392,128]{1,0:T(8,128)} %copy-done.1, f32[392,128]{1,0:T(8,128)} %copy-done.9, ...), custom_call_target="tpu_custom_call" | custom-call | tf_op jit(solution)/shard_map/factorize/pallas_call | solution.py:227
  184.7 16.9 %finish.1 = f32[6272,128]{1,0:T(8,128)} custom-call(s32[2]{0:T(128)} %pad_add_fusion.where_ref, f32[1]{0:T(128)S(6)} %copy.4.damping_ref, bf16[896,896]{1,0:T(8,128)(2,1)} %get-tuple-element.39.high_ref, bf16[896,896]{1,0:T(8,128)(2,1)} %get-tuple-element.40.low_ref, f32[896,896]{1,0:T(8,128)} %get-tuple-element.41.upper_ref, ...), custom_call_target="tpu_custom_call" | custom-call | tf_op jit(solution)/shard_map/finish/pallas_call | solution.py:252
  (83 shorter events, 3.3 us)
Async XLA Ops:
  6.5 132.8 %all-gather.3.cloned.1.call-start = ((), (), s32[]{:S(2)}) async-start(), calls=%async_computation | async-start | bytes 3411968 | tf_op jit(solution)/shard_map/all_gather | solution.py:281
  10.7 3.5 %collective-permute-start.6 = (f32[784,128]{1,0:T(8,128)S(1)}, f32[784,128]{1,0:T(8,128)S(1)}, u32[]{:S(2)}, u32[]{:S(2)}) collective-permute-start(f32[784,128]{1,0:T(8,128)S(1)} %slice.42), channel_id=1, source_target_pairs={{0,224},{1,225},{2,226},{3,227},{4,228},{5,229},{6,230},{7,231},{8... | collective-permute-start | bytes 1204232 | tf_op jit(solution)/shard_map/ppermute | solution.py:275
  11.4 3.5 %collective-permute-start.5 = (f32[784,128]{1,0:T(8,128)S(1)}, f32[784,128]{1,0:T(8,128)S(1)}, u32[]{:S(2)}, u32[]{:S(2)}) collective-permute-start(f32[784,128]{1,0:T(8,128)S(1)} %slice.41), channel_id=1, source_target_pairs={{0,32},{1,33},{2,34},{3,35},{4,36},{5,37},{6,38},{7,39},{8,40},{9,... | collective-permute-start | bytes 1204232 | tf_op jit(solution)/shard_map/ppermute | solution.py:275
  12.1 3.5 %collective-permute-start.4 = (f32[784,128]{1,0:T(8,128)S(1)}, f32[784,128]{1,0:T(8,128)S(1)}, u32[]{:S(2)}, u32[]{:S(2)}) collective-permute-start(f32[784,128]{1,0:T(8,128)S(1)} %slice.40), channel_id=1, source_target_pairs={{0,192},{1,193},{2,194},{3,195},{4,196},{5,197},{6,198},{7,199},{8... | collective-permute-start | bytes 1204232 | tf_op jit(solution)/shard_map/ppermute | solution.py:275
  12.8 2.8 %collective-permute-start.3 = (f32[784,128]{1,0:T(8,128)S(1)}, f32[784,128]{1,0:T(8,128)S(1)}, u32[]{:S(2)}, u32[]{:S(2)}) collective-permute-start(f32[784,128]{1,0:T(8,128)S(1)} %slice.39), channel_id=1, source_target_pairs={{0,64},{1,65},{2,66},{3,67},{4,68},{5,69},{6,70},{7,71},{8,72},{9,... | collective-permute-start | bytes 1204232 | tf_op jit(solution)/shard_map/ppermute | solution.py:275
  13.5 2.1 %collective-permute-start.2 = (f32[784,128]{1,0:T(8,128)S(1)}, f32[784,128]{1,0:T(8,128)S(1)}, u32[]{:S(2)}, u32[]{:S(2)}) collective-permute-start(f32[784,128]{1,0:T(8,128)S(1)} %slice.38), channel_id=1, source_target_pairs={{0,160},{1,161},{2,162},{3,163},{4,164},{5,165},{6,166},{7,167},{8... | collective-permute-start | bytes 1204232 | tf_op jit(solution)/shard_map/ppermute | solution.py:275
  14.2 1.4 collective-permute-start.1
  14.9 0.7 collective-permute-start
  15.9 24.5 %collective-permute-start.7 = (f32[392,128]{1,0:T(8,128)S(1)}, f32[392,128]{1,0:T(8,128)S(1)}, u32[]{:S(2)}, u32[]{:S(2)}) collective-permute-start(f32[392,128]{1,0:T(8,128)S(1)} %slice.46), channel_id=1, source_target_pairs={{0,16},{32,48},{64,80},{96,112},{128,144},{160,176},{192,208},{224... | collective-permute-start | bytes 602120 | tf_op jit(solution)/shard_map/ppermute | solution.py:279
  41.1 143.6 %all-gather.5.cloned.1.call-start = ((), (), s32[]{:S(2)}) async-start(), calls=%async_computation.1 | async-start | bytes 3411968 | tf_op jit(solution)/shard_map/all_gather | solution.py:305
  41.2 0.7 collective-permute-start.8
  41.9 0.7 collective-permute-start.9
  42.6 0.7 collective-permute-start.10
  43.4 21.8 %collective-permute-start.11 = (f32[392,128]{1,0:T(8,128)S(1)}, f32[392,128]{1,0:T(8,128)S(1)}, u32[]{:S(2)}, u32[]{:S(2)}) collective-permute-start(f32[392,128]{1,0:T(8,128)S(1)} %add.47), channel_id=1, source_target_pairs={{0,1},{2,3},{4,5},{6,7},{8,9},{10,11},{12,13},{14,15},{16,17},{18,... | collective-permute-start | bytes 602120 | tf_op jit(solution)/shard_map/ppermute | solution.py:287
  65.2 74.2 %copy-start.1 = (f32[392,128]{1,0:T(8,128)}, f32[392,128]{1,0:T(8,128)S(1)}, u32[]{:S(2)}) copy-start(f32[392,128]{1,0:T(8,128)S(1)} %add.48.refs_0_) | copy-start | bytes 602116
  65.2 6.9 %collective-permute-start.15 = (f32[392,128]{1,0:T(8,128)S(1)}, f32[392,128]{1,0:T(8,128)S(1)}, u32[]{:S(2)}, u32[]{:S(2)}) collective-permute-start(f32[392,128]{1,0:T(8,128)S(1)} %add.48.refs_0_), channel_id=1, source_target_pairs={{0,224},{16,240},{32,0},{48,16},{64,32},{80,48},{96,64},{112,80},{... | collective-permute-start | bytes 602120 | tf_op jit(solution)/shard_map/ppermute | solution.py:290
  72.1 67.3 %copy-start.3 = (f32[392,128]{1,0:T(8,128)}, f32[392,128]{1,0:T(8,128)S(1)}, u32[]{:S(2)}) copy-start(f32[392,128]{1,0:T(8,128)S(1)} %collective-permute-done.15.refs_4_) | copy-start | bytes 602116
  72.1 8.3 %collective-permute-start.19 = (f32[392,128]{1,0:T(8,128)S(1)}, f32[392,128]{1,0:T(8,128)S(1)}, u32[]{:S(2)}, u32[]{:S(2)}) collective-permute-start(f32[392,128]{1,0:T(8,128)S(1)} %collective-permute-done.15.refs_4_), channel_id=1, source_target_pairs={{0,224},{16,240},{32,0},{48,16},{64,32},{80,48},{96,64},{112,80},{... | collective-permute-start | bytes 602120 | tf_op jit(solution)/shard_map/ppermute | solution.py:290
  74.9 24.3 %collective-permute-start.24 = (f32[392,128]{1,0:T(8,128)}, f32[392,128]{1,0:T(8,128)S(1)}, u32[]{:S(2)}, u32[]{:S(2)}) collective-permute-start(f32[392,128]{1,0:T(8,128)} %get-tuple-element.46), channel_id=1, source_target_pairs={{0,0},{1,16},{2,32},{3,48},{4,64},{5,80},{6,96},{7,112},{8,128},{9... | collective-permute-start | bytes 602120 | tf_op jit(solution)/shard_map/ppermute | solution.py:283
  80.4 18.8 %collective-permute-start.23 = (f32[392,128]{1,0:T(8,128)S(1)}, f32[392,128]{1,0:T(8,128)S(1)}, u32[]{:S(2)}, u32[]{:S(2)}) collective-permute-start(f32[392,128]{1,0:T(8,128)S(1)} %collective-permute-done.19.refs_8_), channel_id=1, source_target_pairs={{0,224},{16,240},{32,0},{48,16},{64,32},{80,48},{96,64},{112,80},{... | collective-permute-start | bytes 602120 | tf_op jit(solution)/shard_map/ppermute | solution.py:290
  99.9 5.9 %collective-permute-start.13 = (f32[392,128]{1,0:T(8,128)S(1)}, f32[392,128]{1,0:T(8,128)S(1)}, u32[]{:S(2)}, u32[]{:S(2)}) collective-permute-start(f32[392,128]{1,0:T(8,128)S(1)} %add.48.refs_0_), channel_id=1, source_target_pairs={{0,32},{16,48},{32,64},{48,80},{64,96},{80,112},{96,128},{112,144}... | collective-permute-start | bytes 602120 | tf_op jit(solution)/shard_map/ppermute | solution.py:290
  105.8 7.9 %collective-permute-start.17 = (f32[392,128]{1,0:T(8,128)S(1)}, f32[392,128]{1,0:T(8,128)S(1)}, u32[]{:S(2)}, u32[]{:S(2)}) collective-permute-start(f32[392,128]{1,0:T(8,128)S(1)} %collective-permute-done.13.refs_2_), channel_id=1, source_target_pairs={{0,32},{16,48},{32,64},{48,80},{64,96},{80,112},{96,128},{112,144}... | collective-permute-start | bytes 602120 | tf_op jit(solution)/shard_map/ppermute | solution.py:290
  113.7 9.1 %collective-permute-start.21 = (f32[392,128]{1,0:T(8,128)S(1)}, f32[392,128]{1,0:T(8,128)S(1)}, u32[]{:S(2)}, u32[]{:S(2)}) collective-permute-start(f32[392,128]{1,0:T(8,128)S(1)} %collective-permute-done.17.refs_6_), channel_id=1, source_target_pairs={{0,32},{16,48},{32,64},{48,80},{64,96},{80,112},{96,128},{112,144}... | collective-permute-start | bytes 602120 | tf_op jit(solution)/shard_map/ppermute | solution.py:290
  113.7 17.4 %collective-permute-start.12 = (f32[392,128]{1,0:T(8,128)S(1)}, f32[392,128]{1,0:T(8,128)S(1)}, u32[]{:S(2)}, u32[]{:S(2)}) collective-permute-start(f32[392,128]{1,0:T(8,128)S(1)} %add.48.refs_0_), channel_id=1, source_target_pairs={{0,16},{16,0},{32,48},{48,32},{64,80},{80,64},{96,112},{112,96},{1... | collective-permute-start | bytes 602120 | tf_op jit(solution)/shard_map/ppermute | solution.py:290
  122.3 8.8 %collective-permute-start.14 = (f32[392,128]{1,0:T(8,128)S(1)}, f32[392,128]{1,0:T(8,128)S(1)}, u32[]{:S(2)}, u32[]{:S(2)}) collective-permute-start(f32[392,128]{1,0:T(8,128)S(1)} %collective-permute-done.13.refs_2_), channel_id=1, source_target_pairs={{0,16},{16,0},{32,48},{48,32},{64,80},{80,64},{96,112},{112,96},{1... | collective-permute-start | bytes 602120 | tf_op jit(solution)/shard_map/ppermute | solution.py:290
  122.4 9.2 %collective-permute-start.16 = (f32[392,128]{1,0:T(8,128)S(1)}, f32[392,128]{1,0:T(8,128)S(1)}, u32[]{:S(2)}, u32[]{:S(2)}) collective-permute-start(f32[392,128]{1,0:T(8,128)S(1)} %collective-permute-done.15.refs_4_), channel_id=1, source_target_pairs={{0,16},{16,0},{32,48},{48,32},{64,80},{80,64},{96,112},{112,96},{1... | collective-permute-start | bytes 602120 | tf_op jit(solution)/shard_map/ppermute | solution.py:290
  122.9 8.9 %collective-permute-start.26 = (f32[392,128]{1,0:T(8,128)S(1)}, f32[392,128]{1,0:T(8,128)S(1)}, u32[]{:S(2)}, u32[]{:S(2)}) collective-permute-start(f32[392,128]{1,0:T(8,128)S(1)} %collective-permute-done.21.refs_10_), channel_id=1, source_target_pairs={{0,32},{16,48},{32,64},{48,80},{64,96},{80,112},{96,128},{112,144}... | collective-permute-start | bytes 602120 | tf_op jit(solution)/shard_map/ppermute | solution.py:290
  122.9 16.4 %collective-permute-start.18 = (f32[392,128]{1,0:T(8,128)S(1)}, f32[392,128]{1,0:T(8,128)S(1)}, u32[]{:S(2)}, u32[]{:S(2)}) collective-permute-start(f32[392,128]{1,0:T(8,128)S(1)} %collective-permute-done.17.refs_6_), channel_id=1, source_target_pairs={{0,16},{16,0},{32,48},{48,32},{64,80},{80,64},{96,112},{112,96},{1... | collective-permute-start | bytes 602120 | tf_op jit(solution)/shard_map/ppermute | solution.py:290
  131.1 8.2 %collective-permute-start.20 = (f32[392,128]{1,0:T(8,128)S(1)}, f32[392,128]{1,0:T(8,128)S(1)}, u32[]{:S(2)}, u32[]{:S(2)}) collective-permute-start(f32[392,128]{1,0:T(8,128)S(1)} %collective-permute-done.19.refs_8_), channel_id=1, source_target_pairs={{0,16},{16,0},{32,48},{48,32},{64,80},{80,64},{96,112},{112,96},{1... | collective-permute-start | bytes 602120 | tf_op jit(solution)/shard_map/ppermute | solution.py:290
  131.2 8.1 %collective-permute-start.25 = (f32[392,128]{1,0:T(8,128)S(1)}, f32[392,128]{1,0:T(8,128)S(1)}, u32[]{:S(2)}, u32[]{:S(2)}) collective-permute-start(f32[392,128]{1,0:T(8,128)S(1)} %collective-permute-done.23.refs_12_), channel_id=1, source_target_pairs={{0,16},{16,0},{32,48},{48,32},{64,80},{80,64},{96,112},{112,96},{1... | collective-permute-start | bytes 602120 | tf_op jit(solution)/shard_map/ppermute | solution.py:290
  131.6 7.7 %collective-permute-start.22 = (f32[392,128]{1,0:T(8,128)S(1)}, f32[392,128]{1,0:T(8,128)S(1)}, u32[]{:S(2)}, u32[]{:S(2)}) collective-permute-start(f32[392,128]{1,0:T(8,128)S(1)} %collective-permute-done.21.refs_10_), channel_id=1, source_target_pairs={{0,16},{16,0},{32,48},{48,32},{64,80},{80,64},{96,112},{112,96},{1... | collective-permute-start | bytes 602120 | tf_op jit(solution)/shard_map/ppermute | solution.py:290
  131.7 7.6 %collective-permute-start.27 = (f32[392,128]{1,0:T(8,128)S(1)}, f32[392,128]{1,0:T(8,128)S(1)}, u32[]{:S(2)}, u32[]{:S(2)}) collective-permute-start(f32[392,128]{1,0:T(8,128)S(1)} %collective-permute-done.26.refs_14_), channel_id=1, source_target_pairs={{0,16},{16,0},{32,48},{48,32},{64,80},{80,64},{96,112},{112,96},{1... | collective-permute-start | bytes 602120 | tf_op jit(solution)/shard_map/ppermute | solution.py:290
  (16 other events, 216.1 us)
Sparse Core Ops, SparseCore 0:
  41.3 40.7 all-gather.2
  100.0 58.3 all-gather.4

commit v6 on v5

--- a/solution.py
+++ b/solution.py
@@ -267,12 +267,13 @@
     chips = GRID // 2
     size = own.shape[0] // chips
 
-    piece = jnp.where(row == 0, own[:size], 0.0)
     arrived = []
     source = own
     for z in SCATTER:
         part, source = lax.optimization_barrier((source[size * z:size * (z + 1)], source))
         arrived.append(lax.ppermute(part, "row", [(0, 2 * z)]))
+    source, arrived[0] = lax.optimization_barrier((own, arrived[0]))
+    piece = jnp.where(row == 0, source[:size], 0.0)
     for other in arrived:
         piece = piece + other
 
@@ -297,7 +298,7 @@
     for hop in range(1, chips // 2):
         ahead = step(ahead, forth)
         behind = step(behind, back)
-        if hop == 3:
+        if hop == 2:
             behind, turned = lax.optimization_barrier((behind, turned))
         pieces += [ahead, step(ahead, across), behind, step(behind, across)]
     ahead = step(ahead, forth)

time: 209 us -> 209 us (level)
  the two profiles are of different devices: /device:TPU:139 before, /device:TPU:9 now
where the time goes in v6:
time: 209 us
  waiting for transfers between devices  93.7 us (45%)
  Pallas kernels  61.4 us (29%)
  starting transfers between devices  25 us (12%)
  between operations  14.4 us (7%)
  local copies, waits for them, and re-layouts  9.79 us (5%)
  other arithmetic  4.25 us (2%)
    ppermute x15, waiting for transfers between devices, step(): return lax.ppermute(value, 'row', pairs)  52.8 us
    pallas_call x1, Pallas kernels, factorize(): pl.pallas_call(factor_kernel, out_shape=[jax.ShapeDtypeStruct((ORDER, ORD...  44.5 us
    ppermute x1, waiting for transfers between devices, spread(): lax.ppermute(piece[size // 2:], 'row', [(2 * z, 2 * z + 1) for z in range...  21.2 us
    ppermute x4, waiting for transfers between devices, spread(): lax.ppermute(moving, 'col', [(c, c + hop) for c in range(0, GRID, 2 * hop)])  19.7 us
    pallas_call x1, Pallas kernels, finish(): pl.pallas_call(update_kernel, out_shape=jax.ShapeDtypeStruct((FLAT, LANES...  16.9 us
    ppermute x15, starting transfers between devices, step(): return lax.ppermute(value, 'row', pairs)  10.3 us
    ppermute x7, starting transfers between devices, spread(): arrived.append(lax.ppermute(part, 'row', [(0, 2 * z)]))  8.44 us
    slice x7, local copies, waits for them, and re-layouts, spread(): source[size * z:size * (z + 1)]  8.21 us
  transfers between devices with their start and end apart: 30, of which 8 were waited for; matrix products, arithmetic and copies ran while one was open for 0% of the time, Pallas kernels for 21%

profile of v6, /device:TPU:9, one launch (start us, length us, event | category | flops | bytes accessed | tf_op | source)
XLA Modules:
  0.0 208.5 jit_solution(3518115082097658360)
XLA Ops:
  6.5 1.3 slice.33
  7.8 1.8 slice.36
  9.6 1.8 slice.37
  11.4 1.8 slice.38
  13.2 0.8 slice.39
  14.0 0.8 slice.40
  14.8 0.7 collective-permute-start.6
  16.1 1.4 collective-permute-start.5
  17.6 1.4 collective-permute-start.4
  19.0 1.4 collective-permute-start.3
  20.4 1.4 collective-permute-start.2
  21.8 1.4 collective-permute-start.1
  23.3 1.9 add_add_fusion
  25.2 0.7 copy-done.1
  25.9 1.3 collective-permute-start.7
  27.2 21.2 %collective-permute-done.7 = f32[392,128]{1,0:T(8,128)S(1)} collective-permute-done((f32[392,128]{1,0:T(8,128)S(1)}, f32[392,128]{1,0:T(8,128)S(1)}, u32[]{:S(2)}, u32[]{:S(2)}) %collective-permute-start.7) | collective-permute-done | bytes 200736 | tf_op jit(solution)/shard_map/ppermute | solution.py:280
  48.5 1.6 broadcast_select_fusion
  52.3 1.3 collective-permute-start.11
  53.6 19.7 %collective-permute-done.11 = f32[392,128]{1,0:T(8,128)S(1)} collective-permute-done((f32[392,128]{1,0:T(8,128)S(1)}, f32[392,128]{1,0:T(8,128)S(1)}, u32[]{:S(2)}, u32[]{:S(2)}) %collective-permute-start.11) | collective-permute-done | bytes 200736 | tf_op jit(solution)/shard_map/ppermute | solution.py:288
  73.5 1.6 collective-permute-start.20
  75.0 8.4 %collective-permute-done.15.refs_4_ = f32[392,128]{1,0:T(8,128)S(1)} collective-permute-done((f32[392,128]{1,0:T(8,128)S(1)}, f32[392,128]{1,0:T(8,128)S(1)}, u32[]{:S(2)}, u32[]{:S(2)}) %collective-permute-start.15) | collective-permute-done | bytes 200736 | tf_op jit(solution)/shard_map/ppermute | solution.py:291
  83.4 2.2 %collective-permute-start.19 = (f32[392,128]{1,0:T(8,128)S(1)}, f32[392,128]{1,0:T(8,128)S(1)}, u32[]{:S(2)}, u32[]{:S(2)}) collective-permute-start(f32[392,128]{1,0:T(8,128)S(1)} %collective-permute-done.15.refs_4_), channel_id=1, source_target_pairs={{0,224},{16,240},{32,0},{48,16},{64,32},{80,48},{96,64},{112,80},{... | collective-permute-start | bytes 602120 | tf_op jit(solution)/shard_map/ppermute | solution.py:291
  85.6 18.4 %collective-permute-done.19.refs_8_ = f32[392,128]{1,0:T(8,128)S(1)} collective-permute-done((f32[392,128]{1,0:T(8,128)S(1)}, f32[392,128]{1,0:T(8,128)S(1)}, u32[]{:S(2)}, u32[]{:S(2)}) %collective-permute-start.19) | collective-permute-done | bytes 200736 | tf_op jit(solution)/shard_map/ppermute | solution.py:291
  104.1 10.0 %collective-permute-done.13.refs_2_ = f32[392,128]{1,0:T(8,128)S(1)} collective-permute-done((f32[392,128]{1,0:T(8,128)S(1)}, f32[392,128]{1,0:T(8,128)S(1)}, u32[]{:S(2)}, u32[]{:S(2)}) %collective-permute-start.13) | collective-permute-done | bytes 200736 | tf_op jit(solution)/shard_map/ppermute | solution.py:291
  114.1 8.0 %collective-permute-done.17.refs_6_ = f32[392,128]{1,0:T(8,128)S(1)} collective-permute-done((f32[392,128]{1,0:T(8,128)S(1)}, f32[392,128]{1,0:T(8,128)S(1)}, u32[]{:S(2)}, u32[]{:S(2)}) %collective-permute-start.17) | collective-permute-done | bytes 200736 | tf_op jit(solution)/shard_map/ppermute | solution.py:291
  123.0 3.0 %collective-permute-start.24 = (f32[392,128]{1,0:T(8,128)S(1)}, f32[392,128]{1,0:T(8,128)S(1)}, u32[]{:S(2)}, u32[]{:S(2)}) collective-permute-start(f32[392,128]{1,0:T(8,128)S(1)} %collective-permute-done.19.refs_8_), channel_id=1, source_target_pairs={{0,224},{16,240},{32,0},{48,16},{64,32},{80,48},{96,64},{112,80},{... | collective-permute-start | bytes 602120 | tf_op jit(solution)/shard_map/ppermute | solution.py:291
  125.9 3.5 %collective-permute-done.22.refs_10_ = f32[392,128]{1,0:T(8,128)S(1)} collective-permute-done((f32[392,128]{1,0:T(8,128)S(1)}, f32[392,128]{1,0:T(8,128)S(1)}, u32[]{:S(2)}, u32[]{:S(2)}) %collective-permute-start.22) | collective-permute-done | bytes 200736 | tf_op jit(solution)/shard_map/ppermute | solution.py:291
  129.5 1.3 collective-permute-start.21
  131.5 4.5 %collective-permute-done.26.refs_14_ = f32[392,128]{1,0:T(8,128)S(1)} collective-permute-done((f32[392,128]{1,0:T(8,128)S(1)}, f32[392,128]{1,0:T(8,128)S(1)}, u32[]{:S(2)}, u32[]{:S(2)}) %collective-permute-start.26) | collective-permute-done | bytes 200736 | tf_op jit(solution)/shard_map/ppermute | solution.py:291
  136.0 2.1 %collective-permute-start.27 = (f32[392,128]{1,0:T(8,128)S(1)}, f32[392,128]{1,0:T(8,128)S(1)}, u32[]{:S(2)}, u32[]{:S(2)}) collective-permute-start(f32[392,128]{1,0:T(8,128)S(1)} %collective-permute-done.26.refs_14_), channel_id=1, source_target_pairs={{0,16},{16,0},{32,48},{48,32},{64,80},{80,64},{96,112},{112,96},{1... | collective-permute-start | bytes 602120 | tf_op jit(solution)/shard_map/ppermute | solution.py:291
  140.3 44.5 %factorize.1 = (bf16[896,896]{1,0:T(8,128)(2,1)}, bf16[896,896]{1,0:T(8,128)(2,1)}, f32[896,896]{1,0:T(8,128)}, bf16[896,896]{1,0:T(8,128)(2,1)}, bf16[896,896]{1,0:T(8,128)(2,1)}) custom-call(s32[2]{0:T(128)} %pad_add_fusion.where_ref, f32[1]{0:T(128)S(6)} %copy.4.damping_ref, f32[392,128]{1,0:T(8,128)} %copy-done.2, f32[392,128]{1,0:T(8,128)} %copy-done.11, ...), custom_call_target="tpu_custom_call" | custom-call | tf_op jit(solution)/shard_map/factorize/pallas_call | solution.py:227
  184.8 16.9 %finish.1 = f32[6272,128]{1,0:T(8,128)} custom-call(s32[2]{0:T(128)} %pad_add_fusion.where_ref, f32[1]{0:T(128)S(6)} %copy.4.damping_ref, bf16[896,896]{1,0:T(8,128)(2,1)} %get-tuple-element.43.high_ref, bf16[896,896]{1,0:T(8,128)(2,1)} %get-tuple-element.44.low_ref, f32[896,896]{1,0:T(8,128)} %get-tuple-element.45.upper_ref, ...), custom_call_target="tpu_custom_call" | custom-call | tf_op jit(solution)/shard_map/finish/pallas_call | solution.py:252
  (89 shorter events, 6.2 us)
Async XLA Ops:
  6.5 132.9 %all-gather.3.cloned.1.call-start = ((), (), s32[]{:S(2)}) async-start(), calls=%async_computation | async-start | bytes 3411968 | tf_op jit(solution)/shard_map/all_gather | solution.py:282
  14.8 5.6 %collective-permute-start.6 = (f32[784,128]{1,0:T(8,128)S(1)}, f32[784,128]{1,0:T(8,128)S(1)}, u32[]{:S(2)}, u32[]{:S(2)}) collective-permute-start(f32[784,128]{1,0:T(8,128)S(1)} %slice.41), channel_id=1, source_target_pairs={{0,224},{1,225},{2,226},{3,227},{4,228},{5,229},{6,230},{7,231},{8... | collective-permute-start | bytes 1204232 | tf_op jit(solution)/shard_map/ppermute | solution.py:274
  15.5 6.4 %collective-permute-start = (f32[784,128]{1,0:T(8,128)S(1)}, f32[784,128]{1,0:T(8,128)S(1)}, u32[]{:S(2)}, u32[]{:S(2)}) collective-permute-start(f32[784,128]{1,0:T(8,128)S(1)} %bitcast.13), channel_id=1, source_target_pairs={{0,128},{1,129},{2,130},{3,131},{4,132},{5,133},{6,134},{7,135},{8... | collective-permute-start | bytes 1204232 | tf_op jit(solution)/shard_map/ppermute | solution.py:274
  16.1 7.1 %collective-permute-start.5 = (f32[784,128]{1,0:T(8,128)}, f32[784,128]{1,0:T(8,128)}, u32[]{:S(2)}, u32[]{:S(2)}) collective-permute-start(f32[784,128]{1,0:T(8,128)} %slice.40), channel_id=1, source_target_pairs={{0,32},{1,33},{2,34},{3,35},{4,36},{5,37},{6,38},{7,39},{8,40},{9,... | collective-permute-start | bytes 1204232 | tf_op jit(solution)/shard_map/ppermute | solution.py:274
  17.6 5.7 %collective-permute-start.4 = (f32[784,128]{1,0:T(8,128)}, f32[784,128]{1,0:T(8,128)}, u32[]{:S(2)}, u32[]{:S(2)}) collective-permute-start(f32[784,128]{1,0:T(8,128)} %slice.39), channel_id=1, source_target_pairs={{0,192},{1,193},{2,194},{3,195},{4,196},{5,197},{6,198},{7,199},{8... | collective-permute-start | bytes 1204232 | tf_op jit(solution)/shard_map/ppermute | solution.py:274
  19.0 4.3 %collective-permute-start.3 = (f32[784,128]{1,0:T(8,128)}, f32[784,128]{1,0:T(8,128)}, u32[]{:S(2)}, u32[]{:S(2)}) collective-permute-start(f32[784,128]{1,0:T(8,128)} %slice.38), channel_id=1, source_target_pairs={{0,64},{1,65},{2,66},{3,67},{4,68},{5,69},{6,70},{7,71},{8,72},{9,... | collective-permute-start | bytes 1204232 | tf_op jit(solution)/shard_map/ppermute | solution.py:274
  20.4 2.9 %collective-permute-start.2 = (f32[784,128]{1,0:T(8,128)}, f32[784,128]{1,0:T(8,128)}, u32[]{:S(2)}, u32[]{:S(2)}) collective-permute-start(f32[784,128]{1,0:T(8,128)} %slice.37), channel_id=1, source_target_pairs={{0,160},{1,161},{2,162},{3,163},{4,164},{5,165},{6,166},{7,167},{8... | collective-permute-start | bytes 1204232 | tf_op jit(solution)/shard_map/ppermute | solution.py:274
  21.8 1.5 collective-permute-start.1
  25.9 22.5 %collective-permute-start.7 = (f32[392,128]{1,0:T(8,128)S(1)}, f32[392,128]{1,0:T(8,128)S(1)}, u32[]{:S(2)}, u32[]{:S(2)}) collective-permute-start(f32[392,128]{1,0:T(8,128)S(1)} %slice.45), channel_id=1, source_target_pairs={{0,16},{32,48},{64,80},{96,112},{128,144},{160,176},{192,208},{224... | collective-permute-start | bytes 602120 | tf_op jit(solution)/shard_map/ppermute | solution.py:280
  50.1 134.7 %all-gather.5.cloned.1.call-start = ((), (), s32[]{:S(2)}) async-start(), calls=%async_computation.1 | async-start | bytes 3411968 | tf_op jit(solution)/shard_map/all_gather | solution.py:306
  50.2 0.7 collective-permute-start.8
  50.9 0.7 collective-permute-start.9
  51.6 0.7 collective-permute-start.10
  52.3 21.0 %collective-permute-start.11 = (f32[392,128]{1,0:T(8,128)S(1)}, f32[392,128]{1,0:T(8,128)S(1)}, u32[]{:S(2)}, u32[]{:S(2)}) collective-permute-start(f32[392,128]{1,0:T(8,128)S(1)} %add.47), channel_id=1, source_target_pairs={{0,1},{2,3},{4,5},{6,7},{8,9},{10,11},{12,13},{14,15},{16,17},{18,... | collective-permute-start | bytes 602120 | tf_op jit(solution)/shard_map/ppermute | solution.py:288
  73.3 66.1 %copy-start.2 = (f32[392,128]{1,0:T(8,128)}, f32[392,128]{1,0:T(8,128)S(1)}, u32[]{:S(2)}) copy-start(f32[392,128]{1,0:T(8,128)S(1)} %add.48.refs_0_) | copy-start | bytes 602116
  73.4 10.1 %collective-permute-start.15 = (f32[392,128]{1,0:T(8,128)S(1)}, f32[392,128]{1,0:T(8,128)S(1)}, u32[]{:S(2)}, u32[]{:S(2)}) collective-permute-start(f32[392,128]{1,0:T(8,128)S(1)} %add.48.refs_0_), channel_id=1, source_target_pairs={{0,224},{16,240},{32,0},{48,16},{64,32},{80,48},{96,64},{112,80},{... | collective-permute-start | bytes 602120 | tf_op jit(solution)/shard_map/ppermute | solution.py:291
  73.5 12.2 %collective-permute-start.20 = (f32[392,128]{1,0:T(8,128)}, f32[392,128]{1,0:T(8,128)S(1)}, u32[]{:S(2)}, u32[]{:S(2)}) collective-permute-start(f32[392,128]{1,0:T(8,128)} %get-tuple-element.50), channel_id=1, source_target_pairs={{0,0},{1,16},{2,32},{3,48},{4,64},{5,80},{6,96},{7,112},{8,128},{9... | collective-permute-start | bytes 602120 | tf_op jit(solution)/shard_map/ppermute | solution.py:284
  83.4 56.0 %copy-start.6 = (f32[392,128]{1,0:T(8,128)}, f32[392,128]{1,0:T(8,128)S(1)}, u32[]{:S(2)}) copy-start(f32[392,128]{1,0:T(8,128)S(1)} %collective-permute-done.15.refs_4_) | copy-start | bytes 602116
  83.4 20.6 %collective-permute-start.19 = (f32[392,128]{1,0:T(8,128)S(1)}, f32[392,128]{1,0:T(8,128)S(1)}, u32[]{:S(2)}, u32[]{:S(2)}) collective-permute-start(f32[392,128]{1,0:T(8,128)S(1)} %collective-permute-done.15.refs_4_), channel_id=1, source_target_pairs={{0,224},{16,240},{32,0},{48,16},{64,32},{80,48},{96,64},{112,80},{... | collective-permute-start | bytes 602120 | tf_op jit(solution)/shard_map/ppermute | solution.py:291
  104.0 10.1 %collective-permute-start.13 = (f32[392,128]{1,0:T(8,128)S(1)}, f32[392,128]{1,0:T(8,128)S(1)}, u32[]{:S(2)}, u32[]{:S(2)}) collective-permute-start(f32[392,128]{1,0:T(8,128)S(1)} %add.48.refs_0_), channel_id=1, source_target_pairs={{0,32},{16,48},{32,64},{48,80},{64,96},{80,112},{96,128},{112,144}... | collective-permute-start | bytes 602120 | tf_op jit(solution)/shard_map/ppermute | solution.py:291
  114.1 8.0 %collective-permute-start.17 = (f32[392,128]{1,0:T(8,128)S(1)}, f32[392,128]{1,0:T(8,128)S(1)}, u32[]{:S(2)}, u32[]{:S(2)}) collective-permute-start(f32[392,128]{1,0:T(8,128)S(1)} %collective-permute-done.13.refs_2_), channel_id=1, source_target_pairs={{0,32},{16,48},{32,64},{48,80},{64,96},{80,112},{96,128},{112,144}... | collective-permute-start | bytes 602120 | tf_op jit(solution)/shard_map/ppermute | solution.py:291
  122.1 7.4 %collective-permute-start.22 = (f32[392,128]{1,0:T(8,128)S(1)}, f32[392,128]{1,0:T(8,128)S(1)}, u32[]{:S(2)}, u32[]{:S(2)}) collective-permute-start(f32[392,128]{1,0:T(8,128)S(1)} %collective-permute-done.17.refs_6_), channel_id=1, source_target_pairs={{0,32},{16,48},{32,64},{48,80},{64,96},{80,112},{96,128},{112,144}... | collective-permute-start | bytes 602120 | tf_op jit(solution)/shard_map/ppermute | solution.py:291
  122.1 7.4 %collective-permute-start.12 = (f32[392,128]{1,0:T(8,128)S(1)}, f32[392,128]{1,0:T(8,128)S(1)}, u32[]{:S(2)}, u32[]{:S(2)}) collective-permute-start(f32[392,128]{1,0:T(8,128)S(1)} %add.48.refs_0_), channel_id=1, source_target_pairs={{0,16},{16,0},{32,48},{48,32},{64,80},{80,64},{96,112},{112,96},{1... | collective-permute-start | bytes 602120 | tf_op jit(solution)/shard_map/ppermute | solution.py:291
  122.5 8.3 %collective-permute-start.14 = (f32[392,128]{1,0:T(8,128)S(1)}, f32[392,128]{1,0:T(8,128)S(1)}, u32[]{:S(2)}, u32[]{:S(2)}) collective-permute-start(f32[392,128]{1,0:T(8,128)S(1)} %collective-permute-done.13.refs_2_), channel_id=1, source_target_pairs={{0,16},{16,0},{32,48},{48,32},{64,80},{80,64},{96,112},{112,96},{1... | collective-permute-start | bytes 602120 | tf_op jit(solution)/shard_map/ppermute | solution.py:291
  122.6 8.3 %collective-permute-start.16 = (f32[392,128]{1,0:T(8,128)S(1)}, f32[392,128]{1,0:T(8,128)S(1)}, u32[]{:S(2)}, u32[]{:S(2)}) collective-permute-start(f32[392,128]{1,0:T(8,128)S(1)} %collective-permute-done.15.refs_4_), channel_id=1, source_target_pairs={{0,16},{16,0},{32,48},{48,32},{64,80},{80,64},{96,112},{112,96},{1... | collective-permute-start | bytes 602120 | tf_op jit(solution)/shard_map/ppermute | solution.py:291
  123.0 8.3 %collective-permute-start.24 = (f32[392,128]{1,0:T(8,128)S(1)}, f32[392,128]{1,0:T(8,128)S(1)}, u32[]{:S(2)}, u32[]{:S(2)}) collective-permute-start(f32[392,128]{1,0:T(8,128)S(1)} %collective-permute-done.19.refs_8_), channel_id=1, source_target_pairs={{0,224},{16,240},{32,0},{48,16},{64,32},{80,48},{96,64},{112,80},{... | collective-permute-start | bytes 602120 | tf_op jit(solution)/shard_map/ppermute | solution.py:291
  129.5 6.5 %collective-permute-start.26 = (f32[392,128]{1,0:T(8,128)S(1)}, f32[392,128]{1,0:T(8,128)S(1)}, u32[]{:S(2)}, u32[]{:S(2)}) collective-permute-start(f32[392,128]{1,0:T(8,128)S(1)} %collective-permute-done.22.refs_10_), channel_id=1, source_target_pairs={{0,32},{16,48},{32,64},{48,80},{64,96},{80,112},{96,128},{112,144}... | collective-permute-start | bytes 602120 | tf_op jit(solution)/shard_map/ppermute | solution.py:291
  129.5 9.9 %collective-permute-start.21 = (f32[392,128]{1,0:T(8,128)S(1)}, f32[392,128]{1,0:T(8,128)S(1)}, u32[]{:S(2)}, u32[]{:S(2)}) collective-permute-start(f32[392,128]{1,0:T(8,128)S(1)} %collective-permute-done.19.refs_8_), channel_id=1, source_target_pairs={{0,16},{16,0},{32,48},{48,32},{64,80},{80,64},{96,112},{112,96},{1... | collective-permute-start | bytes 602120 | tf_op jit(solution)/shard_map/ppermute | solution.py:291
  130.8 8.5 %collective-permute-start.18 = (f32[392,128]{1,0:T(8,128)S(1)}, f32[392,128]{1,0:T(8,128)S(1)}, u32[]{:S(2)}, u32[]{:S(2)}) collective-permute-start(f32[392,128]{1,0:T(8,128)S(1)} %collective-permute-done.17.refs_6_), channel_id=1, source_target_pairs={{0,16},{16,0},{32,48},{48,32},{64,80},{80,64},{96,112},{112,96},{1... | collective-permute-start | bytes 602120 | tf_op jit(solution)/shard_map/ppermute | solution.py:291
  130.9 8.4 %collective-permute-start.23 = (f32[392,128]{1,0:T(8,128)S(1)}, f32[392,128]{1,0:T(8,128)S(1)}, u32[]{:S(2)}, u32[]{:S(2)}) collective-permute-start(f32[392,128]{1,0:T(8,128)S(1)} %collective-permute-done.22.refs_10_), channel_id=1, source_target_pairs={{0,16},{16,0},{32,48},{48,32},{64,80},{80,64},{96,112},{112,96},{1... | collective-permute-start | bytes 602120 | tf_op jit(solution)/shard_map/ppermute | solution.py:291
  131.3 8.0 %collective-permute-start.25 = (f32[392,128]{1,0:T(8,128)S(1)}, f32[392,128]{1,0:T(8,128)S(1)}, u32[]{:S(2)}, u32[]{:S(2)}) collective-permute-start(f32[392,128]{1,0:T(8,128)S(1)} %collective-permute-done.24.refs_12_), channel_id=1, source_target_pairs={{0,16},{16,0},{32,48},{48,32},{64,80},{80,64},{96,112},{112,96},{1... | collective-permute-start | bytes 602120 | tf_op jit(solution)/shard_map/ppermute | solution.py:291
  136.0 3.4 %collective-permute-start.27 = (f32[392,128]{1,0:T(8,128)S(1)}, f32[392,128]{1,0:T(8,128)S(1)}, u32[]{:S(2)}, u32[]{:S(2)}) collective-permute-start(f32[392,128]{1,0:T(8,128)S(1)} %collective-permute-done.26.refs_14_), channel_id=1, source_target_pairs={{0,16},{16,0},{32,48},{48,32},{64,80},{80,64},{96,112},{112,96},{1... | collective-permute-start | bytes 602120 | tf_op jit(solution)/shard_map/ppermute | solution.py:291
  (19 other events, 160.0 us)
Sparse Core Ops, SparseCore 0:
  50.2 54.9 all-gather.2
  107.8 50.9 all-gather.4
